TPU v7x, 128 devices: a whole 4x4x4 slice. The times are simulated.
128 devices in a mesh: gx: 16 (over z, x), gy: 8 (over y, core).
Axes of the slice: x: 4, y: 4, z: 4, core: 2. Of those that a mesh axis runs over, the one named last changes fastest.
Arguments:
- velocity: float32 [3, 256, 256, 128], P(None, 'gx', 'gy'), may hold values from -3 to 3
- theta: float32 [256, 256, 128], P('gx', 'gy'), may hold values from -4 to 4
- vapour: float32 [256, 256, 128], P('gx', 'gy'), may hold values from 0.5 to 1.5
- radius_sq: float32 [64, 4096], P(None, ('gx', 'gy')), may hold values from 0.5 to 2
- multiplicity: float32 [64, 4096], P(None, ('gx', 'gy')), may hold values from 0.5 to 2
- counts: int32 [4096], P(('gx', 'gy')), may hold values from 16 to 64
- pairing: int32 [4096, 64], P(('gx', 'gy')), may hold values from 0 to 63, each once within a row
- destination: int32 [64, 4096], P(None, ('gx', 'gy')), may hold values from 0 to 4095
Outputs:
- velocity_new: float32 [3, 256, 256, 128], P(None, 'gx', 'gy')
- theta_new: float32 [256, 256, 128], P('gx', 'gy')
- vapour_new: float32 [256, 256, 128], P('gx', 'gy')
- moments: float32 [3, 4096], P(None, ('gx', 'gy'))
Inputs may be any that keep to these rules, and one draw needn't show every extreme that they name: `pairing`: each row is a permutation of 0 to 63.
All inputs are finite; a program needn't handle non-finite values.
Results may differ from a plain program's by a relative error of at most 0.0003.
Values sent between devices are 32-bit elements; how exact they have to be, the bound alone decides.
A program may use at most 64 MiB of HBM per device.

v0:
```python
import math

import jax
import jax.numpy as jnp
from jax import lax
from jax.sharding import PartitionSpec as P

BW = 4


TIME_STEP = 0.2
DIFFUSION = 0.05
BUOYANCY = 0.5
GROWTH = 0.5
COLLISION = 0.05
CONDENSE = 0.002
HIGHEST = lax.Precision.HIGHEST


def extended(shard, sides, width):
    for axis, dim in sides:
        count, length = (lax.axis_size(axis), shard.shape[dim])
        up = [(i, (i + 1) % count) for i in range(count)]
        down = [(j, i) for i, j in up]
        last = lax.slice_in_dim(shard, length - width, length, axis=dim)
        initial = lax.slice_in_dim(shard, 0, width, axis=dim)
        before = lax.ppermute(last, axis, up)
        after = lax.ppermute(initial, axis, down)
        shard = jnp.concatenate([before, shard, after], axis=dim)
    return shard


def from_behind(block, axis, distance):
    devices = range(lax.axis_size(axis))
    route = [((i - distance) % len(devices), i) for i in devices]
    return lax.ppermute(block, axis, route)


def vertical_pair(values):
    upper_cell = jnp.concatenate([values[..., 1:], values[..., -1:]], axis=-1)
    lower_cell = jnp.concatenate([values[..., :1], values[..., :-1]], axis=-1)
    return (upper_cell, lower_cell)


def advect_fields(centre, east_cell, west_cell, north_cell, south_cell):
    upper_cell, lower_cell = vertical_pair(centre)
    carried = -0.5 * (
        centre[0] * (east_cell - west_cell)
        + centre[1] * (north_cell - south_cell)
        + centre[2] * (upper_cell - lower_cell)
    )
    spread = (
        east_cell + west_cell + north_cell + south_cell + upper_cell + lower_cell - 6.0 * centre
    )
    return centre + TIME_STEP * (carried + DIFFUSION * spread)


def cosine_table(levels):
    level_index = jnp.arange(levels).astype(jnp.float32)
    return jnp.cos(math.pi * (level_index[:, None] + 0.5) * level_index[None, :] / levels)


def fourier_table(length, blocks, block_width):
    wave_index = jnp.arange(length)
    positions = jnp.arange(blocks)[:, None] * block_width + jnp.arange(block_width)[None, :]
    residue = wave_index[:, None, None] * positions[None] % length
    angles = 2.0 * math.pi / length * residue.astype(jnp.float32)
    return (jnp.cos(angles), jnp.sin(angles))


def forward_planes(planes, cosine_x, sine_x, cosine_y, sine_y):
    real_x = jnp.einsum("kai,mabij->mkbj", cosine_x, planes, precision=HIGHEST)
    imag_x = -jnp.einsum("kai,mabij->mkbj", sine_x, planes, precision=HIGHEST)
    real_xy = jnp.einsum("lbj,mkbj->mkl", cosine_y, real_x, precision=HIGHEST) + jnp.einsum(
        "lbj,mkbj->mkl", sine_y, imag_x, precision=HIGHEST
    )
    imag_xy = jnp.einsum("lbj,mkbj->mkl", cosine_y, imag_x, precision=HIGHEST) - jnp.einsum(
        "lbj,mkbj->mkl", sine_y, real_x, precision=HIGHEST
    )
    return (real_xy, imag_xy)


def solve_modes(real_xy, imag_xy, first_mode, levels):
    mode_count, span_kx, span_ky = real_xy.shape
    mode_index = first_mode + jnp.arange(mode_count)
    wave_x = 2.0 * jnp.cos(2.0 * math.pi * jnp.arange(span_kx).astype(jnp.float32) / span_kx) - 2.0
    wave_y = 2.0 * jnp.cos(2.0 * math.pi * jnp.arange(span_ky).astype(jnp.float32) / span_ky) - 2.0
    wave_z = 2.0 * jnp.cos(math.pi * mode_index.astype(jnp.float32) / levels) - 2.0
    eigenvalue = wave_x[None, :, None] + wave_y[None, None, :] + wave_z[:, None, None]
    anchor = (
        (mode_index == 0)[:, None, None]
        & (jnp.arange(span_kx) == 0)[None, :, None]
        & (jnp.arange(span_ky) == 0)[None, None, :]
    )
    safe_value = jnp.where(anchor, 1.0, eigenvalue)
    return (
        jnp.where(anchor, 0.0, real_xy / safe_value),
        jnp.where(anchor, 0.0, imag_xy / safe_value),
    )


def inverse_planes(real_part, imag_part, cosine_x, sine_x, cosine_y, sine_y):
    real_y = jnp.einsum("lbj,fmkl->fmkbj", cosine_y, real_part, precision=HIGHEST) - jnp.einsum(
        "lbj,fmkl->fmkbj", sine_y, imag_part, precision=HIGHEST
    )
    imag_y = jnp.einsum("lbj,fmkl->fmkbj", sine_y, real_part, precision=HIGHEST) + jnp.einsum(
        "lbj,fmkl->fmkbj", cosine_y, imag_part, precision=HIGHEST
    )
    summed = jnp.einsum("kai,fmkbj->fmabij", cosine_x, real_y, precision=HIGHEST) - jnp.einsum(
        "kai,fmkbj->fmabij", sine_x, imag_y, precision=HIGHEST
    )
    return summed / (cosine_x.shape[0] * cosine_y.shape[0])


def shards(velocity, theta, vapour, radius_sq, multiplicity, counts, pairing, destination):
    span_x, span_y, levels = theta.shape
    grid_x = lax.axis_size("gx")
    grid_y = lax.axis_size("gy")
    device_count = grid_x * grid_y
    rank_x = lax.axis_index("gx")
    rank_y = lax.axis_index("gy")
    stacked = jnp.concatenate([velocity, theta[None], vapour[None]], axis=0)
    widened = extended(stacked, (("gx", 1), ("gy", 2)), 2)
    centre = widened[:, 1 : span_x + 2, 1 : span_y + 2]
    east_cell = widened[:, 2 : span_x + 3, 1 : span_y + 2]
    west_cell = widened[:, 0 : span_x + 1, 1 : span_y + 2]
    north_cell = widened[:, 1 : span_x + 2, 2 : span_y + 3]
    south_cell = widened[:, 1 : span_x + 2, 0 : span_y + 1]
    wide_advected = advect_fields(centre, east_cell, west_cell, north_cell, south_cell)
    wide_x = wide_advected[0]
    wide_y = wide_advected[1]
    star_z = wide_advected[2, 1:, 1:] + TIME_STEP * BUOYANCY * centre[3, 1:, 1:]
    below_z = jnp.concatenate([jnp.zeros_like(star_z[..., :1]), star_z[..., :-1]], axis=-1)
    divergence = (
        wide_x[1:, 1:] - wide_x[:-1, 1:] + (wide_y[1:, 1:] - wide_y[1:, :-1]) + (star_z - below_z)
    )
    advected = wide_advected[:, 1:, 1:]
    star_x = advected[0]
    star_y = advected[1]
    level_table = cosine_table(levels)
    spectral = jnp.einsum("ijz,zm->mij", divergence, level_table, precision=HIGHEST).reshape(
        levels, 1, span_x, span_y
    )
    planes = lax.all_to_all(spectral, ("gx", "gy"), split_axis=0, concat_axis=1, tiled=True)
    per_device = levels // device_count
    planes = planes.reshape(per_device, grid_x, grid_y, span_x, span_y)
    total_x = span_x * grid_x
    total_y = span_y * grid_y
    cosine_x, sine_x = fourier_table(total_x, grid_x, span_x)
    cosine_y, sine_y = fourier_table(total_y, grid_y, span_y)
    real_xy, imag_xy = forward_planes(planes, cosine_x, sine_x, cosine_y, sine_y)
    device_rank = rank_x * grid_y + rank_y
    real_xy, imag_xy = solve_modes(real_xy, imag_xy, device_rank * per_device, levels)
    weight = jnp.where(jnp.arange(levels) == 0, 1.0 / levels, 2.0 / levels)
    back_table = level_table * weight[None, :]
    single = inverse_planes(real_xy[None], imag_xy[None], cosine_x, sine_x, cosine_y, sine_y)
    single = single.reshape(1, per_device, device_count, span_x, span_y)
    returned = lax.all_to_all(
        single, ("gx", "gy"), split_axis=2, concat_axis=1, tiled=True
    ).reshape(levels, span_x, span_y)
    pressure = jnp.einsum("mij,zm->ijz", returned, back_table, precision=HIGHEST)
    next_plane = from_behind(pressure[0:1], "gx", -1)
    step_east = jnp.concatenate([pressure[1:], next_plane], axis=0) - pressure
    next_row = from_behind(pressure[:, 0:1], "gy", -1)
    step_north = jnp.concatenate([pressure[:, 1:], next_row], axis=1) - pressure
    step_up = jnp.concatenate([pressure[..., 1:], pressure[..., -1:]], axis=-1) - pressure
    velocity_new = jnp.stack([star_x - step_east, star_y - step_north, star_z - step_up])
    theta_new = advected[3]
    moist_field = advected[4]
    box_x = span_x // BW
    box_y = span_y // BW
    box_count = box_x * box_y
    slot_count = radius_sq.shape[0]
    column_sums = moist_field.reshape(box_x, BW, box_y, BW, levels).sum(axis=(1, 3, 4))
    box_mean = (column_sums / (BW * BW * levels)).reshape(box_count)
    slot_index = jnp.arange(slot_count)[:, None]
    live_weight = jnp.where(slot_index < counts[None, :], multiplicity, 0.0)
    grown_sq = radius_sq + GROWTH * jax.nn.softplus(box_mean)[None, :]
    mass_before = radius_sq * jnp.sqrt(radius_sq)
    mass_grown = grown_sq * jnp.sqrt(grown_sq)
    condensed = jnp.sum(live_weight * (mass_grown - mass_before), axis=0)
    vapour_new = (
        moist_field.reshape(box_x, BW, box_y, BW, levels)
        - CONDENSE * condensed.reshape(box_x, 1, box_y, 1, 1)
    ).reshape(span_x, span_y, levels)
    half_count = slot_count // 2
    one_hot = (pairing.T[:, None, :] == jnp.arange(slot_count)[None, :, None]).astype(jnp.float32)
    paired = jnp.einsum(
        "kib,kjb->ijb", one_hot[:half_count], one_hot[half_count:], precision=HIGHEST
    )
    paired = paired + jnp.transpose(paired, (1, 0, 2))
    radius_now = jnp.sqrt(grown_sq)
    radius_sum = radius_now[:, None, :] + radius_now[None, :, :]
    rate_tile = (
        radius_sum
        * radius_sum
        * jnp.abs(grown_sq[:, None, :] - grown_sq[None, :, :])
        * live_weight[None, :, :]
        * paired
    )
    collide_rate = jnp.sum(rate_tile, axis=1)
    gained = jnp.sum(rate_tile * mass_grown[None, :, :], axis=1)
    mass_final = (mass_grown + COLLISION * gained) / (1.0 + COLLISION * collide_rate)
    local_box = jnp.arange(box_count)
    source_x = rank_x * box_x + local_box // box_y
    source_y = rank_y * box_y + local_box % box_y
    target_device = destination // box_count
    target_local = destination % box_count
    target_x = target_device // grid_y * box_x + target_local // box_y
    target_y = target_device % grid_y * box_y + target_local % box_y
    offset_x = (target_x - source_x[None, :] + 1) % (box_x * grid_x) - 1
    offset_y = (target_y - source_y[None, :] + 1) % (box_y * grid_y) - 1
    carried_load = jnp.stack(
        [live_weight, live_weight * mass_final, live_weight * mass_final * mass_final]
    )
    packed = jnp.concatenate(
        [carried_load, offset_x[None].astype(jnp.float32), offset_y[None].astype(jnp.float32)],
        axis=0,
    )
    packed = packed.reshape(5, slot_count, box_x, box_y)
    bordered = extended(packed, (("gx", 2), ("gy", 3)), 1)
    arrived = jnp.zeros((3, box_x, box_y), jnp.float32)
    for step_x in (-1, 0, 1):
        for step_y in (-1, 0, 1):
            source = bordered[
                :, :, 1 - step_x : 1 - step_x + box_x, 1 - step_y : 1 - step_y + box_y
            ]
            chosen = ((source[3] == step_x) & (source[4] == step_y)).astype(jnp.float32)
            arrived = arrived + jnp.sum(source[:3] * chosen[None], axis=1)
    moments = arrived.reshape(3, box_count) / slot_count
    return (velocity_new, theta_new, vapour_new, moments)


def solution(mesh):
    placed = (
        P(None, "gx", "gy", None),
        P("gx", "gy", None),
        P("gx", "gy", None),
        P(None, ("gx", "gy")),
        P(None, ("gx", "gy")),
        P(("gx", "gy")),
        P(("gx", "gy"), None),
        P(None, ("gx", "gy")),
    )
    return jax.shard_map(
        shards,
        mesh=mesh,
        in_specs=placed,
        out_specs=(
            P(None, "gx", "gy", None),
            P("gx", "gy", None),
            P("gx", "gy", None),
            P(None, ("gx", "gy")),
        ),
        check_vma=False,
    )
```

profile of v0, /device:TPU:1, one launch (start us, length us, event | category | flops | bytes accessed | tf_op | source)
XLA Modules:
  0.0 106.9 jit_solution(13865165558095613117)
XLA Ops:
  0.7 1.8 %pad_maximum_fusion.11 = (f32[5,2,32,128]{3,2,1,0:T(8,128)}, f32[5,2,32,128]{3,2,1,0:T(8,128)}) fusion(f32[1,16,32,128]{3,2,1,0:T(8,128)} %bitcast.205, f32[1,16,32,128]{3,2,1,0:T(8,128)} %bitcast.201, f32[3,16,32,128]{3,2,1,0:T(8,128)} %param.8), kind=kLoop, calls=%fused_computation.100 | loop fusion | flops 163840 | bytes 1638400 | tf_op jit(solution)/shard_map/slice | solution.py:25
  2.4 2.0 %collective-permute-start = (f32[5,2,32,128]{3,2,1,0:T(8,128)}, f32[5,2,32,128]{3,2,1,0:T(8,128)S(1)}, u32[]{:S(2)}, u32[]{:S(2)}) collective-permute-start(f32[5,2,32,128]{3,2,1,0:T(8,128)} %get-tuple-element.38), channel_id=1, source_target_pairs={{0,8},{8,16},{16,24},{24,32},{32,40},{40,48},{48,56},{56,64},{64,7... | collective-permute-start | bytes 491528 | tf_op jit(solution)/shard_map/ppermute | solution.py:27
  4.5 4.7 %collective-permute-start.1 = (f32[5,2,32,128]{3,2,1,0:T(8,128)}, f32[5,2,32,128]{3,2,1,0:T(8,128)S(1)}, u32[]{:S(2)}, u32[]{:S(2)}) collective-permute-start(f32[5,2,32,128]{3,2,1,0:T(8,128)} %get-tuple-element.39), channel_id=1, source_target_pairs={{8,0},{16,8},{24,16},{32,24},{40,32},{48,40},{56,48},{64,56},{72,6... | collective-permute-start | bytes 491528 | tf_op jit(solution)/shard_map/ppermute | solution.py:28
  9.2 0.6 multiply_add_fusion.1
  9.8 1.1 iota_compare_fusion
  10.9 0.5 fusion.13
  11.6 1.9 %fusion.53 = (f32[256,8,32]{0,2,1:T(8,128)S(1)}, f32[256,8,32]{0,2,1:T(8,128)}) fusion(s32[8,32]{1,0:T(8,128)S(1)} %iota_add_fusion.1), kind=kLoop, calls=%fused_computation.105 | loop fusion | flops 917504 | bytes 525312 | tf_op jit(solution)/shard_map/sin | solution.py:68
  13.5 0.7 and_convert_fusion
  14.2 0.6 iota_convert_fusion
  14.8 1.3 %copy.25 = f32[32,64,64]{1,2,0:T(8,128)} copy(f32[32,64,64]{2,1,0:T(8,128)S(1)} %fusion.13) | data formatting | bytes 1048576 | tf_op jit(solution)/shard_map/kib,kjb->ijb/dot_general | solution.py:188
  16.2 0.6 iota_compare_fusion.2
  16.9 2.1 %collective-permute-start.2 = (f32[5,20,2,128]{3,2,1,0:T(2,128)S(1)}, f32[5,20,2,128]{3,2,1,0:T(2,128)S(1)}, u32[]{:S(2)}, u32[]{:S(2)}) collective-permute-start(f32[5,20,2,128]{3,2,1,0:T(2,128)S(1)} %get-tuple-element.37), channel_id=1, source_target_pairs={{0,1},{1,2},{2,3},{3,4},{4,5},{5,6},{6,7},{7,0},{8,9},{9,10},{10,1... | collective-permute-start | bytes 307208 | tf_op jit(solution)/shard_map/ppermute | solution.py:27
  19.1 0.5 compare_select_fusion.1
  19.5 1.2 %collective-permute-done.2 = f32[5,20,2,128]{3,2,1,0:T(2,128)S(1)} collective-permute-done((f32[5,20,2,128]{3,2,1,0:T(2,128)S(1)}, f32[5,20,2,128]{3,2,1,0:T(2,128)S(1)}, u32[]{:S(2)}, u32[]{:S(2)}) %collective-permute-start.2) | collective-permute-done | bytes 102432 | tf_op jit(solution)/shard_map/ppermute | solution.py:27
  20.7 0.3 maximum_maximum_fusion
  21.0 0.6 fusion.163
  21.6 0.6 fusion.164
  22.4 1.2 %collective-permute-done.3 = f32[5,20,2,128]{3,2,1,0:T(2,128)S(1)} collective-permute-done((f32[5,20,2,128]{3,2,1,0:T(2,128)S(1)}, f32[5,20,2,128]{3,2,1,0:T(2,128)S(1)}, u32[]{:S(2)}, u32[]{:S(2)}) %collective-permute-start.3) | collective-permute-done | bytes 102432 | tf_op jit(solution)/shard_map/ppermute | solution.py:28
  23.6 2.9 %multiply_add_fusion = f32[5,17,33,128]{3,2,1,0:T(8,128)S(1)} fusion(f32[5,20,34,128]{3,2,1,0:T(8,128)S(1)} %maximum_maximum_fusion, f32[5,17,33,127]{3,2,1,0:T(8,128)S(1)} %get-tuple-element.25, f32[5,17,33,1]{3,2,1,0:T(8,128)S(1)} %get-tuple-element.27, f32[5,17,33,1]{3,2,1,0:T(8,128)S(1)} %get-tuple-element.26, ...), kind=kLoop, calls=%fused_computation.8 | loop fusion | flops 9694080 | bytes 12655616 | tf_op jit(solution)/shard_map/add | solution.py:55
  26.5 0.9 slice_reduce_fusion
  27.5 0.3 copy-done.1
  27.8 0.9 slice_bitcast_fusion.1
  29.1 2.6 %multiply_reduce_fusion = (f32[64,32]{0,1:T(8,128)S(1)}, f32[64,32]{0,1:T(8,128)S(1)}) fusion(f32[64,32]{0,1:T(8,128)S(1)} %get-tuple-element.57, f32[32,64,64]{2,1,0:T(8,128)S(1)} %fusion.13, f32[32,64,64]{1,2,0:T(8,128)} %copy.25, f32[64,32]{0,1:T(8,128)S(1)} %get-tuple-element.20, f32[64,32]{0,1:T(8,128)S(1)} %get-tuple-element.58, ...), kind=kLoop, calls=%fused_computation.31 | loop fusion | flops 1437696 | bytes 1097728 | tf_op jit(solution)/shard_map/reduce_sum | solution.py:202
  32.0 0.7 bitcast_dynamic-update-slice_fusion.1
  32.7 0.7 bitcast_dynamic-update-slice_fusion
  33.5 0.6 fusion.165
  34.1 4.8 %collective-permute-start.7 = (f32[5,64,1,8]{1,3,2,0:T(8,128)S(1)}, f32[5,64,1,8]{1,3,2,0:T(8,128)S(1)}, u32[]{:S(2)}, u32[]{:S(2)}) collective-permute-start(f32[5,64,1,8]{1,3,2,0:T(8,128)S(1)} %get-tuple-element.54), channel_id=1, source_target_pairs={{8,0},{16,8},{24,16},{32,24},{40,32},{48,40},{56,48},{64,56},{72,6... | collective-permute-start | bytes 30728 | tf_op jit(solution)/shard_map/ppermute | solution.py:28
  39.1 0.9 bitcast_subtract_fusion
  40.0 1.4 %convolution_bitcast_fusion.6 = f32[128,1,16,32]{0,3,2,1:T(8,128)} fusion(f32[17,33,128]{2,1,0:T(8,128)S(1)} %copy-done.7, f32[17,33,128]{2,1,0:T(8,128)S(1)} %copy-done.6, f32[16,32,128]{2,1,0:T(8,128)S(1)} %get-tuple-element.31, f32[16,32,127]{2,1,0:T(8,128)S(1)} %bitcast.211, f32[128]{0:T(128)S(1)} %copy-done.15, f32[128]{0:T(128)S(1)} %add_multiply_fusion.1), kind=kOutput, calls=%fused_computation.20 | convolution fusion | flops 101023744 | bytes 1836032 | tf_op jit(solution)/shard_map/ijz,zm->mij/dot_general | solution.py:141
  41.4 1.5 %copy.21 = f32[128,1,16,32]{3,2,1,0:T(8,128)S(1)} copy(f32[128,1,16,32]{0,3,2,1:T(8,128)} %convolution_bitcast_fusion.6) | data formatting | bytes 524288 | tf_op jit(solution)/shard_map/reshape | solution.py:141
  42.8 1.2 %reshape.346 = f32[128,1,512]{2,1,0:T(1,128)} reshape(f32[128,1,16,32]{3,2,1,0:T(8,128)S(1)} %copy.21) | data formatting | bytes 524288
  44.0 5.4 %all-to-all-start = ((f32[128,1,512]{2,1,0:T(1,128)}), f32[128,1,512]{2,1,0:T(1,128)S(1)}, u32[]{:S(2)}, u32[]{:S(2)}) async-start(f32[128,1,512]{2,1,0:T(1,128)} %reshape.346), calls=%async_computation | async-start | bytes 524288 | tf_op jit(solution)/shard_map/all_to_all | solution.py:144
  49.5 1.2 %collective-permute-start.8 = (f32[5,64,6,1]{1,3,2,0:T(1,128)S(1)}, f32[5,64,6,1]{1,3,2,0:T(1,128)S(1)}, u32[]{:S(2)}, u32[]{:S(2)}) collective-permute-start(f32[5,64,6,1]{1,3,2,0:T(1,128)S(1)} %get-tuple-element.49), channel_id=1, source_target_pairs={{1,0},{2,1},{3,2},{4,3},{5,4},{6,5},{7,6},{0,7},{9,8},{10,9},{11,1... | collective-permute-start | bytes 23048 | tf_op jit(solution)/shard_map/ppermute | solution.py:28
  50.8 0.5 collective-permute-start.9
  51.5 1.5 %collective-permute-done.8 = f32[5,64,6,1]{1,3,2,0:T(1,128)S(1)} collective-permute-done((f32[5,64,6,1]{1,3,2,0:T(1,128)S(1)}, f32[5,64,6,1]{1,3,2,0:T(1,128)S(1)}, u32[]{:S(2)}, u32[]{:S(2)}) %collective-permute-start.8) | collective-permute-done | bytes 7712 | tf_op jit(solution)/shard_map/ppermute | solution.py:28
  53.1 0.3 collective-permute-done.9
  53.4 0.8 pad_maximum_fusion.8
  54.3 6.1 %all-to-all-done = f32[128,1,512]{2,1,0:T(1,128)S(1)} async-done(((f32[128,1,512]{2,1,0:T(1,128)}), f32[128,1,512]{2,1,0:T(1,128)S(1)}, u32[]{:S(2)}, u32[]{:S(2)}) %all-to-all-start) | async-done | bytes 262176 | tf_op jit(solution)/shard_map/all_to_all | solution.py:144
  60.4 0.6 broadcast.404
  61.0 2.0 %reduce.3 = f32[128,512]{1,0:T(8,128)} reduce(f32[128,1,512]{2,1,0:T(1,128)S(1)} %all-to-all-done, f32[]{:T(128)} %broadcast.404), dimensions={1}, to_apply=%all_to_all.4.reduce_sub_computation | reduce | bytes 524292 | tf_op jit(solution)/shard_map/all_to_all | solution.py:144
  63.1 1.2 %reshape.347 = f32[128,1,16,32]{3,2,1,0:T(8,128)S(1)} reshape(f32[128,512]{1,0:T(8,128)} %reduce.3) | data formatting | bytes 524288
  64.3 2.7 %convolution_bitcast_fusion.5 = f32[256,8,32]{0,2,1:T(8,128)S(1)} fusion(s32[16,16]{1,0:T(8,128)S(1)} %iota_add_fusion, f32[16,8,16,32]{3,2,1,0:T(8,128)S(1)} %bitcast.199), kind=kOutput, calls=%fused_computation.19 | convolution fusion | flops 202244096 | bytes 525312 | tf_op jit(solution)/shard_map/kai,mabij->mkbj/dot_general | solution.py:72
  67.0 1.5 %convolution_bitcast_fusion = f32[256,256]{1,0:T(8,128)S(1)} fusion(f32[256,8,32]{0,2,1:T(8,128)S(1)} %convolution_bitcast_fusion.5, s32[8,32]{1,0:T(8,128)S(1)} %iota_add_fusion.1), kind=kOutput, calls=%fused_computation.12 | convolution fusion | flops 202244096 | bytes 525312 | tf_op jit(solution)/shard_map/lbj,mkbj->mkl/dot_general | solution.py:77
  68.5 2.7 %fusion.3 = f32[256,8,32]{0,2,1:T(8,128)S(1)} fusion(s32[16,16]{1,0:T(8,128)S(1)} %iota_add_fusion, f32[16,8,16,32]{3,2,1,0:T(8,128)S(1)} %bitcast.200), kind=kOutput, calls=%fused_computation.18 | convolution fusion | flops 202309632 | bytes 525312 | tf_op jit(solution)/shard_map/kai,mabij->mkbj/dot_general | solution.py:73
  71.2 1.5 %convolution_bitcast_fusion.2 = f32[256,256]{1,0:T(8,128)S(1)} fusion(f32[256,8,32]{0,2,1:T(8,128)S(1)} %fusion.3, s32[8,32]{1,0:T(8,128)S(1)} %iota_add_fusion.1), kind=kOutput, calls=%fused_computation.14 | convolution fusion | flops 202244096 | bytes 525312 | tf_op jit(solution)/shard_map/lbj,mkbj->mkl/dot_general | solution.py:74
  72.8 1.5 %fusion.9 = f32[256,256]{1,0:T(8,128)S(1)} fusion(f32[256,256]{1,0:T(8,128)S(1)} %convolution_bitcast_fusion, f32[256,8,32]{0,2,1:T(8,128)S(1)} %fusion.3, f32[]{:T(128)S(6)} %sub.166, f32[256]{0:T(256)S(1)} %copy-done.21, s32[8,32]{1,0:T(8,128)S(1)} %iota_add_fusion.1, pred[256]{0:T(512)(128)(4,1)S(1)} %copy-done.19, pred[256]{0:T(512)(128)(4,1)S(1)} %copy-done.20), kind=kOutput, calls=%fused_computation.26 | convolution fusion | flops 202702848 | bytes 788996 | tf_op jit(solution)/shard_map/lbj,mkbj->mkl/dot_general | solution.py:77
  74.3 1.5 %fusion.6 = f32[256,256]{1,0:T(8,128)S(1)} fusion(f32[256,256]{1,0:T(8,128)S(1)} %convolution_bitcast_fusion.2, f32[256,8,32]{0,2,1:T(8,128)S(1)} %convolution_bitcast_fusion.5, f32[]{:T(128)S(6)} %sub.166, f32[256]{0:T(256)S(1)} %copy-done.21, s32[8,32]{1,0:T(8,128)S(1)} %iota_add_fusion.1, pred[256]{0:T(512)(128)(4,1)S(1)} %copy-done.19, ...), kind=kOutput, calls=%fused_computation.23 | convolution fusion | flops 202702848 | bytes 788996 | tf_op jit(solution)/shard_map/lbj,mkbj->mkl/dot_general | solution.py:74
  75.8 0.6 fusion.167
  76.5 0.4 fusion.169
  76.9 0.4 fusion.166
  77.3 0.4 fusion.168
  77.8 2.0 %fusion.35 = f32[8,32,16,16]{1,3,2,0:T(8,128)S(1)} fusion(f32[256,8,32]{0,2,1:T(8,128)S(1)} %bitcast.219, f32[256,8,32]{0,2,1:T(8,128)S(1)} %bitcast.218, s32[16,16]{1,0:T(8,128)S(1)} %iota_add_fusion), kind=kOutput, calls=%fused_computation.76 | convolution fusion | flops 202309632 | bytes 787456 | tf_op jit(solution)/shard_map/kai,fmkbj->fmabij/dot_general | solution.py:109
  79.8 2.0 %fusion.1 = f32[1,1,16,8,16,32]{5,4,2,3,1,0:T(8,128)S(1)} fusion(f32[8,32,16,16]{1,3,2,0:T(8,128)S(1)} %fusion.35, f32[256,8,32]{0,2,1:T(8,128)S(1)} %bitcast.217, f32[256,8,32]{0,2,1:T(8,128)S(1)} %bitcast.216, s32[16,16]{1,0:T(8,128)S(1)} %iota_add_fusion), kind=kOutput, calls=%fused_computation.11 | convolution fusion | flops 202440704 | bytes 1049600 | tf_op jit(solution)/shard_map/kai,fmkbj->fmabij/dot_general | solution.py:109
  81.9 1.2 %reshape.348 = f32[128,1,512]{2,1,0:T(1,128)} reshape(f32[128,1,1,16,32]{4,3,2,1,0:T(8,128)S(1)} %bitcast.210) | data formatting | bytes 524288
  83.1 4.4 %all-to-all-start.1 = ((f32[128,1,512]{2,1,0:T(1,128)}), f32[128,1,512]{2,1,0:T(1,128)S(1)}, u32[]{:S(2)}, u32[]{:S(2)}) async-start(f32[128,1,512]{2,1,0:T(1,128)} %reshape.348), calls=%async_computation.1 | async-start | bytes 524288 | tf_op jit(solution)/shard_map/all_to_all | solution.py:158
  88.0 10.6 %all-to-all-done.1 = f32[128,1,512]{2,1,0:T(1,128)S(1)} async-done(((f32[128,1,512]{2,1,0:T(1,128)}), f32[128,1,512]{2,1,0:T(1,128)S(1)}, u32[]{:S(2)}, u32[]{:S(2)}) %all-to-all-start.1) | async-done | bytes 262176 | tf_op jit(solution)/shard_map/all_to_all | solution.py:158
  98.5 1.3 %reduce.4 = f32[128,512]{1,0:T(8,128)S(1)} reduce(f32[128,1,512]{2,1,0:T(1,128)S(1)} %all-to-all-done.1, f32[]{:T(128)} %broadcast.404), dimensions={1}, to_apply=%all_to_all.5.reduce_sub_computation | reduce | bytes 524292 | tf_op jit(solution)/shard_map/all_to_all | solution.py:158
  100.1 0.5 copy.24
  100.6 0.7 fusion.39
  101.3 1.3 %collective-permute-start.4 = (f32[1,32,128]{2,1,0:T(8,128)S(1)}, f32[1,32,128]{2,1,0:T(8,128)S(1)}, u32[]{:S(2)}, u32[]{:S(2)}) collective-permute-start(f32[1,32,128]{2,1,0:T(8,128)S(1)} %slice.345), channel_id=1, source_target_pairs={{8,0},{16,8},{24,16},{32,24},{40,32},{48,40},{56,48},{64,56},{72,6... | collective-permute-start | bytes 49160 | tf_op jit(solution)/shard_map/ppermute | solution.py:36
  102.7 0.7 collective-permute-start.5
  103.3 0.6 add_multiply_fusion
  104.2 1.5 %collective-permute-done.5 = f32[16,1,128]{2,1,0:T(1,128)S(1)} collective-permute-done((f32[16,1,128]{2,1,0:T(1,128)S(1)}, f32[16,1,128]{2,1,0:T(1,128)S(1)}, u32[]{:S(2)}, u32[]{:S(2)}) %collective-permute-start.5) | collective-permute-done | bytes 8224 | tf_op jit(solution)/shard_map/ppermute | solution.py:36
  106.0 0.9 pad_maximum_fusion.7
  (97 shorter events, 3.2 us)
Async XLA Ops:
  0.6 12.8 %copy-start.11 = (f32[64,32]{0,1:T(8,128)S(1)}, f32[64,32]{0,1:T(8,128)}, u32[]{:S(2)}) copy-start(f32[64,32]{0,1:T(8,128)} %param.12) | copy-start | bytes 24580
  0.6 12.8 %copy-start.17 = (s32[32]{0:T(128)S(1)}, s32[32]{0:T(128)}, u32[]{:S(2)}) copy-start(s32[32]{0:T(128)} %param.13) | copy-start | bytes 388
  0.7 12.9 %copy-start.12 = (s32[64,32]{0,1:T(8,128)S(1)}, s32[64,32]{0,1:T(8,128)}, u32[]{:S(2)}) copy-start(s32[64,32]{0,1:T(8,128)} %param.15) | copy-start | bytes 24580
  2.4 14.3 %collective-permute-start = (f32[5,2,32,128]{3,2,1,0:T(8,128)}, f32[5,2,32,128]{3,2,1,0:T(8,128)S(1)}, u32[]{:S(2)}, u32[]{:S(2)}) collective-permute-start(f32[5,2,32,128]{3,2,1,0:T(8,128)} %get-tuple-element.38), channel_id=1, source_target_pairs={{0,8},{8,16},{16,24},{24,32},{32,40},{40,48},{48,56},{56,64},{64,7... | collective-permute-start | bytes 491528 | tf_op jit(solution)/shard_map/ppermute | solution.py:27
  4.5 12.3 %collective-permute-start.1 = (f32[5,2,32,128]{3,2,1,0:T(8,128)}, f32[5,2,32,128]{3,2,1,0:T(8,128)S(1)}, u32[]{:S(2)}, u32[]{:S(2)}) collective-permute-start(f32[5,2,32,128]{3,2,1,0:T(8,128)} %get-tuple-element.39), channel_id=1, source_target_pairs={{8,0},{16,8},{24,16},{32,24},{40,32},{48,40},{56,48},{64,56},{72,6... | collective-permute-start | bytes 491528 | tf_op jit(solution)/shard_map/ppermute | solution.py:28
  9.2 30.7 %copy-start.13 = (f32[128]{0:T(128)}, f32[128]{0:T(128)S(1)}, u32[]{:S(2)}) copy-start(f32[128]{0:T(128)S(1)} %add_multiply_fusion.1) | copy-start | bytes 1540
  10.9 5.9 %copy-start = (f32[3,16,32,128]{3,2,1,0:T(8,128)S(1)}, f32[3,16,32,128]{3,2,1,0:T(8,128)}, u32[]{:S(2)}) copy-start(f32[3,16,32,128]{3,2,1,0:T(8,128)} %param.8) | copy-start | bytes 2359300
  10.9 5.9 %copy-start.3 = (f32[16,32,128]{2,1,0:T(8,128)S(1)}, f32[16,32,128]{2,1,0:T(8,128)}, u32[]{:S(2)}) copy-start(f32[16,32,128]{2,1,0:T(8,128)} %param.9) | copy-start | bytes 786436
  10.9 5.9 %copy-start.4 = (f32[16,32,128]{2,1,0:T(8,128)S(1)}, f32[16,32,128]{2,1,0:T(8,128)}, u32[]{:S(2)}) copy-start(f32[16,32,128]{2,1,0:T(8,128)} %param.10) | copy-start | bytes 786436
  16.9 3.8 %collective-permute-start.2 = (f32[5,20,2,128]{3,2,1,0:T(2,128)S(1)}, f32[5,20,2,128]{3,2,1,0:T(2,128)S(1)}, u32[]{:S(2)}, u32[]{:S(2)}) collective-permute-start(f32[5,20,2,128]{3,2,1,0:T(2,128)S(1)} %get-tuple-element.37), channel_id=1, source_target_pairs={{0,1},{1,2},{2,3},{3,4},{4,5},{5,6},{6,7},{7,0},{8,9},{9,10},{10,1... | collective-permute-start | bytes 307208 | tf_op jit(solution)/shard_map/ppermute | solution.py:27
  19.5 4.1 %collective-permute-start.3 = (f32[5,20,2,128]{3,2,1,0:T(2,128)S(1)}, f32[5,20,2,128]{3,2,1,0:T(2,128)S(1)}, u32[]{:S(2)}, u32[]{:S(2)}) collective-permute-start(f32[5,20,2,128]{3,2,1,0:T(2,128)S(1)} %get-tuple-element.36), channel_id=1, source_target_pairs={{1,0},{2,1},{3,2},{4,3},{5,4},{6,5},{7,6},{0,7},{9,8},{10,9},{11,1... | collective-permute-start | bytes 307208 | tf_op jit(solution)/shard_map/ppermute | solution.py:28
  26.5 1.3 %copy-start.1 = (f32[5,17,33,128]{3,2,1,0:T(8,128)}, f32[5,17,33,128]{3,2,1,0:T(8,128)S(1)}, u32[]{:S(2)}) copy-start(f32[5,17,33,128]{3,2,1,0:T(8,128)S(1)} %multiply_add_fusion) | copy-start | bytes 4308484
  26.5 2.5 %copy-start.9 = (f32[64,32]{0,1:T(8,128)S(1)}, f32[64,32]{0,1:T(8,128)}, u32[]{:S(2)}) copy-start(f32[64,32]{0,1:T(8,128)} %param.11) | copy-start | bytes 24580
  28.7 10.4 %copy-start.2 = (f32[5,17,33,128]{3,2,1,0:T(8,128)S(1)}, f32[5,17,33,128]{3,2,1,0:T(8,128)}, u32[]{:S(2)}) copy-start(f32[5,17,33,128]{3,2,1,0:T(8,128)} %copy-done.1) | copy-start | bytes 4308484
  31.8 8.2 %copy-start.6 = (f32[17,33,128]{2,1,0:T(8,128)S(1)}, f32[17,33,128]{2,1,0:T(8,128)}, u32[]{:S(2)}) copy-start(f32[17,33,128]{2,1,0:T(8,128)} %get-tuple-element.34) | copy-start | bytes 861700
  31.8 8.2 %copy-start.7 = (f32[17,33,128]{2,1,0:T(8,128)S(1)}, f32[17,33,128]{2,1,0:T(8,128)}, u32[]{:S(2)}) copy-start(f32[17,33,128]{2,1,0:T(8,128)} %get-tuple-element.35) | copy-start | bytes 861700
  31.8 8.2 %copy-start.15 = (f32[128]{0:T(128)S(1)}, f32[128]{0:T(128)}, u32[]{:S(2)}) copy-start(f32[128]{0:T(128)} %iota_convert_fusion) | copy-start | bytes 1540
  34.1 15.4 %collective-permute-start.6 = (f32[5,64,1,8]{1,3,2,0:T(8,128)}, f32[5,64,1,8]{1,3,2,0:T(8,128)S(1)}, u32[]{:S(2)}, u32[]{:S(2)}) collective-permute-start(f32[5,64,1,8]{1,3,2,0:T(8,128)} %get-tuple-element.53), channel_id=1, source_target_pairs={{0,8},{8,16},{16,24},{24,32},{32,40},{40,48},{48,56},{56,64},{64,7... | collective-permute-start | bytes 30728 | tf_op jit(solution)/shard_map/ppermute | solution.py:27
  34.1 15.4 %collective-permute-start.7 = (f32[5,64,1,8]{1,3,2,0:T(8,128)S(1)}, f32[5,64,1,8]{1,3,2,0:T(8,128)S(1)}, u32[]{:S(2)}, u32[]{:S(2)}) collective-permute-start(f32[5,64,1,8]{1,3,2,0:T(8,128)S(1)} %get-tuple-element.54), channel_id=1, source_target_pairs={{8,0},{16,8},{24,16},{32,24},{40,32},{48,40},{56,48},{64,56},{72,6... | collective-permute-start | bytes 30728 | tf_op jit(solution)/shard_map/ppermute | solution.py:28
  41.4 8.0 %copy-start.10 = (f32[64,32]{0,1:T(8,128)S(1)}, f32[64,32]{0,1:T(8,128)}, u32[]{:S(2)}) copy-start(f32[64,32]{0,1:T(8,128)} %get-tuple-element.14) | copy-start | bytes 24580
  44.0 16.4 %all-to-all-start = ((f32[128,1,512]{2,1,0:T(1,128)}), f32[128,1,512]{2,1,0:T(1,128)S(1)}, u32[]{:S(2)}, u32[]{:S(2)}) async-start(f32[128,1,512]{2,1,0:T(1,128)} %reshape.346), calls=%async_computation | async-start | bytes 524288 | tf_op jit(solution)/shard_map/all_to_all | solution.py:144
  49.5 3.5 %collective-permute-start.8 = (f32[5,64,6,1]{1,3,2,0:T(1,128)S(1)}, f32[5,64,6,1]{1,3,2,0:T(1,128)S(1)}, u32[]{:S(2)}, u32[]{:S(2)}) collective-permute-start(f32[5,64,6,1]{1,3,2,0:T(1,128)S(1)} %get-tuple-element.49), channel_id=1, source_target_pairs={{1,0},{2,1},{3,2},{4,3},{5,4},{6,5},{7,6},{0,7},{9,8},{10,9},{11,1... | collective-permute-start | bytes 23048 | tf_op jit(solution)/shard_map/ppermute | solution.py:28
  50.8 2.6 %collective-permute-start.9 = (f32[5,64,6,1]{1,3,2,0:T(1,128)S(1)}, f32[5,64,6,1]{1,3,2,0:T(1,128)S(1)}, u32[]{:S(2)}, u32[]{:S(2)}) collective-permute-start(f32[5,64,6,1]{1,3,2,0:T(1,128)S(1)} %get-tuple-element.50), channel_id=1, source_target_pairs={{0,1},{1,2},{2,3},{3,4},{4,5},{5,6},{6,7},{7,0},{8,9},{9,10},{10,1... | collective-permute-start | bytes 23048 | tf_op jit(solution)/shard_map/ppermute | solution.py:27
  68.5 4.2 %copy-start.19 = (pred[256]{0:T(512)(128)(4,1)S(1)}, pred[256]{0:T(512)(128)(4,1)}, u32[]{:S(2)}) copy-start(pred[256]{0:T(512)(128)(4,1)} %get-tuple-element.61) | copy-start | bytes 772
  68.5 4.2 %copy-start.20 = (pred[256]{0:T(512)(128)(4,1)S(1)}, pred[256]{0:T(512)(128)(4,1)}, u32[]{:S(2)}) copy-start(pred[256]{0:T(512)(128)(4,1)} %get-tuple-element.62) | copy-start | bytes 772
  68.5 4.2 %copy-start.21 = (f32[256]{0:T(256)S(1)}, f32[256]{0:T(256)}, u32[]{:S(2)}) copy-start(f32[256]{0:T(256)} %multiply_add_fusion.1) | copy-start | bytes 3076
  74.3 2.2 %copy-start.5 = (f32[256,8,32]{0,2,1:T(8,128)S(1)}, f32[256,8,32]{0,2,1:T(8,128)}, u32[]{:S(2)}) copy-start(f32[256,8,32]{0,2,1:T(8,128)} %get-tuple-element.60) | copy-start | bytes 786436
  81.8 5.7 %copy-start.8 = (f32[5,64,6,9]{1,3,2,0:T(8,128)S(1)}, f32[5,64,6,9]{1,3,2,0:T(8,128)}, u32[]{:S(2)}) copy-start(f32[5,64,6,9]{1,3,2,0:T(8,128)} %get-tuple-element.48) | copy-start | bytes 207364
  83.1 15.5 %all-to-all-start.1 = ((f32[128,1,512]{2,1,0:T(1,128)}), f32[128,1,512]{2,1,0:T(1,128)S(1)}, u32[]{:S(2)}, u32[]{:S(2)}) async-start(f32[128,1,512]{2,1,0:T(1,128)} %reshape.348), calls=%async_computation.1 | async-start | bytes 524288 | tf_op jit(solution)/shard_map/all_to_all | solution.py:158
  87.5 13.1 %copy-start.14 = (f32[128]{0:T(128)S(1)}, f32[128]{0:T(128)}, u32[]{:S(2)}) copy-start(f32[128]{0:T(128)} %copy-done.13) | copy-start | bytes 1540
  87.5 13.1 %copy-start.16 = (f32[128]{0:T(128)S(1)}, f32[128]{0:T(128)}, u32[]{:S(2)}) copy-start(f32[128]{0:T(128)} %iota_convert_fusion) | copy-start | bytes 1540
  87.5 13.1 %copy-start.18 = (f32[128]{0:T(128)S(1)}, f32[128]{0:T(128)}, u32[]{:S(2)}) copy-start(f32[128]{0:T(128)} %compare_select_fusion.1) | copy-start | bytes 1540
  101.3 4.4 %collective-permute-start.4 = (f32[1,32,128]{2,1,0:T(8,128)S(1)}, f32[1,32,128]{2,1,0:T(8,128)S(1)}, u32[]{:S(2)}, u32[]{:S(2)}) collective-permute-start(f32[1,32,128]{2,1,0:T(8,128)S(1)} %slice.345), channel_id=1, source_target_pairs={{8,0},{16,8},{24,16},{32,24},{40,32},{48,40},{56,48},{64,56},{72,6... | collective-permute-start | bytes 49160 | tf_op jit(solution)/shard_map/ppermute | solution.py:36
  102.7 3.1 %collective-permute-start.5 = (f32[16,1,128]{2,1,0:T(1,128)S(1)}, f32[16,1,128]{2,1,0:T(1,128)S(1)}, u32[]{:S(2)}, u32[]{:S(2)}) collective-permute-start(f32[16,1,128]{2,1,0:T(1,128)S(1)} %slice.348), channel_id=1, source_target_pairs={{1,0},{2,1},{3,2},{4,3},{5,4},{6,5},{7,6},{0,7},{9,8},{10,9},{11,1... | collective-permute-start | bytes 24584 | tf_op jit(solution)/shard_map/ppermute | solution.py:36
where the time goes:
time: 107 us
  starting transfers between devices  27.3 us (26%)
  waiting for transfers between devices  22.5 us (21%)
  other arithmetic  22.4 us (21%)
  matrix products  19.8 us (19%)
  local copies, waits for them, and re-layouts  13.6 us (13%)
  between operations  1.36 us (1%)
    ppermute x4, starting transfers between devices, extended(): after = lax.ppermute(initial, axis, down)  10.7 us
    all_to_all x1, waiting for transfers between devices, shards(): lax.all_to_all(single, ('gx', 'gy'), split_axis=2, concat_axis=1, tiled=T...  10.6 us
    all_to_all x1, waiting for transfers between devices, shards(): lax.all_to_all(spectral, ('gx', 'gy'), split_axis=0, concat_axis=1, tiled...  6.11 us
    all_to_all x1, starting transfers between devices, shards(): lax.all_to_all(spectral, ('gx', 'gy'), split_axis=0, concat_axis=1, tiled...  5.38 us
    unnamed x49, local copies, waits for them, and re-layouts  4.96 us
    ppermute x4, starting transfers between devices, extended(): before = lax.ppermute(last, axis, up)  4.72 us
    all_to_all x1, starting transfers between devices, shards(): lax.all_to_all(single, ('gx', 'gy'), split_axis=2, concat_axis=1, tiled=T...  4.39 us
    add x1, other arithmetic, advect_fields(): return centre + TIME_STEP * (carried + DIFFUSION * spread)  2.9 us
  transfers between devices with their start and end apart: 12, of which 7 were waited for; matrix products, arithmetic and copies ran while one was open for 16% of the time, Pallas kernels for 0%

commit v1 on v0

v1 whole, which is shorter than its diff:
```python
import functools
import math

import jax
import jax.numpy as jnp
import numpy as np
from jax import lax
from jax.experimental import pallas as pl
from jax.experimental.pallas import tpu as pltpu
from jax.sharding import PartitionSpec as P

MESH = pl.DeviceIdType.MESH
GX, GY = 16, 8
DEV = GX * GY
SX, SY, NZ = 16, 32, 128
NX, NY = 256, 256
HALF = 72
F32 = jnp.float32
BF16 = jnp.bfloat16
ANY = pl.BlockSpec(memory_space=pl.ANY)


def split_table(table):
    table = np.asarray(table, np.float32)
    high = table.astype(jnp.bfloat16)
    low = (table - high.astype(np.float32)).astype(jnp.bfloat16)
    return np.stack([high, low])


@functools.cache
def tables():
    tau = 2.0 * math.pi
    z = np.arange(NZ)
    cosine = np.cos(math.pi * (z[None, :] + 0.5) * z[:, None] / NZ)
    weight = np.where(z == 0, 1.0 / NZ, 2.0 / NZ)
    back = cosine * weight[:, None]
    rows, factor, seen = [], [], set()
    for p in range(16):
        for q in range(8):
            if (p, q) in seen:
                continue
            mirror = (-p % 16, -q % 8)
            seen.update({(p, q), mirror})
            rows.append((p, q))
            factor.append(1.0 if mirror == (p, q) else 2.0)
    pad = HALF - len(rows)
    low_x = np.array([r[0] for r in rows] + [0] * pad)
    low_y = np.array([r[1] for r in rows] + [0] * pad)
    factor = np.array(factor + [0.0] * pad)
    used = np.array([1.0] * len(rows) + [0.0] * pad)
    a = np.repeat(np.arange(16), 8)
    b = np.tile(np.arange(8), 16)
    first, last = [], []
    for c in range(4):
        angle = tau * (
            low_x[:, None] * a[None] / 16.0
            + low_y[:, None] * b[None] / 8.0
            + low_x[:, None] * c / 64.0
        )
        first.append(np.concatenate([np.cos(angle) * used[:, None], -np.sin(angle) * used[:, None]]))
        scale = factor[:, None] / (NX * NY)
        last.append(np.concatenate([np.cos(angle) * scale, -np.sin(angle) * scale]).T)
    lane_i = np.repeat(np.arange(4), 32)
    lane_j = np.tile(np.arange(32), 4)
    turn_cos, turn_sin, wave = [], [], []
    for q in range(4):
        kx0 = low_x + 16 * q
        angle = tau * (kx0[:, None] * lane_i[None] + low_y[:, None] * lane_j[None]) / 256.0
        turn_cos.append(np.cos(angle))
        turn_sin.append(np.sin(angle))
        kx = kx0[:, None] + 64 * lane_i[None]
        ky = low_y[:, None] + 8 * lane_j[None]
        wave.append(-4.0 * np.sin(math.pi * kx / NX) ** 2 - 4.0 * np.sin(math.pi * ky / NY) ** 2)
    turns = np.stack([np.concatenate(turn_cos), np.concatenate(turn_sin), np.concatenate(wave)])
    angle = tau * (lane_i[:, None] * lane_i[None] / 4.0 + lane_j[:, None] * lane_j[None] / 32.0)
    cos2, sin2 = np.cos(angle), np.sin(angle)
    ahead = np.block([[cos2, -sin2], [sin2, cos2]])
    behind = np.block([[cos2, sin2], [-sin2, cos2]])
    wave_z = -4.0 * np.sin(math.pi * z / (2.0 * NZ)) ** 2
    wave_z = np.broadcast_to(wave_z[:, None], (NZ, 128)).astype(np.float32)
    box = np.zeros((32, 128), np.float32)
    for column in range(4):
        for j in range(32):
            box[column * 8 + j // 4, column * 32 + j] = 1.0
    return dict(
        cosine=split_table(cosine),
        first=split_table(np.stack(first)),
        ahead=split_table(ahead),
        behind=split_table(behind),
        last=split_table(np.stack(last)),
        turns=turns.astype(np.float32),
        wave_z=wave_z,
        box=box.astype(jnp.bfloat16),
        back=split_table(back),
    )


def halves(values):
    high = values.astype(BF16)
    return high, (values - high.astype(F32)).astype(BF16)


def product(left, right, dims):
    def one(x, y):
        return lax.dot_general(x, y, (dims, ((), ())), preferred_element_type=F32)

    (left_high, left_low), (right_high, right_low) = left, right
    return one(left_high, right_high) + (one(left_high, right_low) + one(left_low, right_high))


NN = ((1,), (0,))
NT = ((1,), (1,))
TN = ((0,), (0,))


def step_kernel(
    vel, theta, vapour, radius, multi, counts, pairing, dest,
    cosine_h, first_h, ahead_h, behind_h, last_h, turns_h, wave_h, box_h,
    modes, star, theta_out, vapour_out, moments_out,
    fp, ad, xu2, yl, yh, corner, row_y0, below_y, quad, send1, got1, send2,
    cosine, first, ahead, behind, last, turns, wave, box,
    rad_v, mul_v, cnt_v, pair_v, dst_v, cond, load, near, res,
    load_sem, drop_sem, table_sem, hs_sem, hr_sem, s1_sem, r1_sem, s2_sem, r2_sem, own_sem,
    ms_sem, mr_sem, out_sem,
):
    gx = lax.axis_index("gx")
    gy = lax.axis_index("gy")
    me = gx * GY + gy
    east, west = lax.rem(gx + 1, GX), lax.rem(gx + GX - 1, GX)
    north, south = lax.rem(gy + 1, GY), lax.rem(gy + GY - 1, GY)
    peers_y = [lax.rem(gy + r, GY) for r in range(GY)]

    loads = [
        pltpu.make_async_copy(vel, fp.at[pl.ds(0, 3), pl.ds(1, SX)], load_sem.at[0]),
        pltpu.make_async_copy(theta, fp.at[3, pl.ds(1, SX)], load_sem.at[1]),
        pltpu.make_async_copy(vapour, fp.at[4, pl.ds(1, SX)], load_sem.at[2]),
    ]
    drops = [
        pltpu.make_async_copy(source, target, drop_sem.at[k])
        for k, (source, target) in enumerate(
            [(radius, rad_v), (multi, mul_v), (counts, cnt_v), (pairing, pair_v), (dest, dst_v)]
        )
    ]
    table_pairs = [
        (cosine_h, cosine), (box_h, box), (first_h, first), (turns_h, turns), (ahead_h, ahead),
        (wave_h, wave), (behind_h, behind), (last_h, last),
    ]
    fetches = [
        pltpu.make_async_copy(source, target, table_sem.at[k])
        for k, (source, target) in enumerate(table_pairs)
    ]
    for copy in loads + drops + fetches:
        copy.start()

    barrier = pltpu.get_barrier_semaphore()

    def greet(px, ry):
        pl.semaphore_signal(barrier, inc=1, device_id=(px, peers_y[ry]), device_id_type=MESH)

    for ry in range(1, GY):
        greet(gx, ry)

    def greet_column(rx, carry):
        px = lax.rem(gx + rx, GX)
        for ry in range(GY):
            greet(px, ry)
        return carry

    lax.fori_loop(1, GX, greet_column, 0)

    for copy in drops:
        copy.wait()
    slot = lax.broadcasted_iota(jnp.int32, (64, 32), 0)
    live = jnp.where(slot < cnt_v[...][None, :], mul_v[...], 0.0)
    target = dst_v[...]
    local_box = lax.broadcasted_iota(jnp.int32, (64, 32), 1)
    source_x = gx * 4 + (local_box >> 3)
    source_y = gy * 8 + (local_box & 7)
    target_x = (target >> 8) * 4 + ((target & 31) >> 3)
    target_y = ((target >> 5) & 7) * 8 + (target & 7)
    offset_x = (target_x - source_x + 1) & 63
    offset_y = (target_y - source_y + 1) & 63
    code = (offset_x * 3 + offset_y).astype(F32)
    wide = jnp.concatenate([rad_v[...], live, code, jnp.zeros((64, 32), F32)], axis=1)
    flat = jnp.concatenate([wide, wide], axis=0).T
    pair = pair_v[...]
    order = jnp.concatenate([pair, pltpu.roll(jnp.concatenate([pair, pair], axis=1), 32, 1)[:, :64]], axis=1)
    radius_p = jnp.take_along_axis(flat[0:32], order, axis=1)
    live_p = jnp.take_along_axis(flat[32:64], order, axis=1)
    code_p = jnp.take_along_axis(flat[64:96], order, axis=1)

    pl.semaphore_wait(barrier, DEV - 1)

    def remote(source, target_ref, k, device):
        return pltpu.make_async_remote_copy(
            src_ref=source, dst_ref=target_ref, send_sem=hs_sem.at[k], recv_sem=hr_sem.at[k],
            device_id=device, device_id_type=MESH,
        )

    halo = [
        remote(vel.at[:, SX - 1], fp.at[pl.ds(0, 3), 0], 0, (east, gy)),
        remote(theta.at[SX - 1], fp.at[3, 0], 1, (east, gy)),
        remote(vapour.at[SX - 1], fp.at[4, 0], 2, (east, gy)),
        remote(vel.at[0, SX - 2], xu2, 3, (east, gy)),
        remote(vel.at[:, 0], fp.at[pl.ds(0, 3), SX + 1], 4, (west, gy)),
        remote(theta.at[0], fp.at[3, SX + 1], 5, (west, gy)),
        remote(vapour.at[0], fp.at[4, SX + 1], 6, (west, gy)),
        remote(vel.at[:, :, SY - 1], yl.at[pl.ds(0, 3)], 7, (gx, north)),
        remote(theta.at[:, SY - 1], yl.at[3], 8, (gx, north)),
        remote(vapour.at[:, SY - 1], yl.at[4], 9, (gx, north)),
        remote(vel.at[1, :, SY - 2], yl.at[5], 10, (gx, north)),
        remote(vel.at[:, :, 0], yh.at[pl.ds(0, 3)], 11, (gx, south)),
        remote(theta.at[:, 0], yh.at[3], 12, (gx, south)),
        remote(vapour.at[:, 0], yh.at[4], 13, (gx, south)),
        remote(vel.at[0, SX - 1, pl.ds(SY - 1, 1)], corner.at[0, pl.ds(0, 1)], 14, (east, north)),
        remote(vel.at[0, SX - 1, pl.ds(0, 1)], corner.at[1, pl.ds(0, 1)], 15, (east, south)),
        remote(vel.at[1, SX - 1, pl.ds(SY - 1, 1)], corner.at[2, pl.ds(0, 1)], 16, (east, north)),
        remote(vel.at[1, 0, pl.ds(SY - 1, 1)], corner.at[3, pl.ds(0, 1)], 17, (west, north)),
    ]
    for copy in halo:
        copy.start()
    for copy in loads:
        copy.wait()

    row = lax.broadcasted_iota(jnp.int32, (SY, NZ), 0)
    lane = lax.broadcasted_iota(jnp.int32, (SY, NZ), 1)
    tile_row = lax.broadcasted_iota(jnp.int32, (8, NZ), 0)

    def upward(values):
        return pltpu.roll(values, NZ - 1, 1)

    def downward(values):
        return pltpu.roll(values, 1, 1)

    def coefficients(speed, shape_lane=None):
        scaled = 0.1 * speed
        return 0.01 - scaled, 0.01 + scaled

    def vertical(speed, lanes):
        up, down = coefficients(speed)
        top, bottom = lanes == NZ - 1, lanes == 0
        centre = 0.94 + jnp.where(top, up, 0.0) + jnp.where(bottom, down, 0.0)
        return jnp.where(top, 0.0, up), jnp.where(bottom, 0.0, down), centre

    def advect_plane(x):
        c_east, c_west = coefficients(fp[0, x + 1])
        c_north, c_south = coefficients(fp[1, x + 1])
        c_north = jnp.where(row == SY - 1, 0.0, c_north)
        c_south = jnp.where(row == 0, 0.0, c_south)
        c_up, c_down, c_mid = vertical(fp[2, x + 1], lane)
        for f in range(5):
            centre = fp[f, x + 1]
            ad[f, x + 1] = (
                (c_mid * centre + c_east * fp[f, x + 2] + c_west * fp[f, x])
                + (c_north * pltpu.roll(centre, SY - 1, 0) + c_south * pltpu.roll(centre, 1, 0))
                + (c_up * upward(centre) + c_down * downward(centre))
            )
        row_y0[pl.ds(x, 1), :] = fp[1, x + 1, 0:1, :]

    def inner(x, carry):
        advect_plane(x)
        return carry

    lax.fori_loop(1, SX - 1, inner, 0)
    for copy in halo:
        copy.wait_recv()
    advect_plane(0)
    advect_plane(SX - 1)

    speed = fp[0, 0]
    c_east, c_west = coefficients(speed)
    c_north, c_south = coefficients(fp[1, 0])
    c_up, c_down, c_mid = vertical(fp[2, 0], lane)
    above = jnp.where(row == SY - 1, corner[1, 0:1, :], pltpu.roll(speed, SY - 1, 0))
    beneath = jnp.where(row == 0, corner[0, 0:1, :], pltpu.roll(speed, 1, 0))
    ad[0, 0] = (
        (c_mid * speed + c_east * fp[0, 1] + c_west * xu2[...])
        + (c_north * above + c_south * beneath)
        + (c_up * upward(speed) + c_down * downward(speed))
    )
    speed = yl[1]
    row_x = lax.broadcasted_iota(jnp.int32, (SX, NZ), 0)
    lane_x = lax.broadcasted_iota(jnp.int32, (SX, NZ), 1)
    c_east, c_west = coefficients(yl[0])
    c_north, c_south = coefficients(speed)
    c_up, c_down, c_mid = vertical(yl[2], lane_x)
    after = jnp.where(row_x == SX - 1, corner[3, 0:1, :], pltpu.roll(speed, SX - 1, 0))
    before = jnp.where(row_x == 0, corner[2, 0:1, :], pltpu.roll(speed, 1, 0))
    below_y[...] = (
        (c_mid * speed + c_east * after + c_west * before)
        + (c_north * row_y0[...] + c_south * yl[5])
        + (c_up * upward(speed) + c_down * downward(speed))
    )
    fetches[0].wait()

    def block(c, carry):
        total = jnp.zeros((SY, NZ), F32)
        parts = []
        for i in range(4):
            x = c * 4 + i
            _, c_south = coefficients(fp[1, x + 1, 0:8, :])
            c_north, _ = coefficients(fp[1, x + 1, SY - 8 : SY, :])
            c_south = jnp.where(tile_row == 0, c_south, 0.0)
            c_north = jnp.where(tile_row == 7, c_north, 0.0)
            for f in range(5):
                ad[f, x + 1, 0:8, :] += c_south * yl[f, pl.ds(x, 1), :]
                ad[f, x + 1, SY - 8 : SY, :] += c_north * yh[f, pl.ds(x, 1), :]
            star_w = ad[2, x + 1] + 0.1 * fp[3, x + 1]
            ad[2, x + 1] = star_w
            star_v = ad[1, x + 1]
            behind_v = jnp.where(row == 0, below_y[pl.ds(x, 1), :], pltpu.roll(star_v, 1, 0))
            below_w = jnp.where(lane == 0, 0.0, downward(star_w))
            parts.append((ad[0, x + 1] - ad[0, x]) + (star_v - behind_v) + (star_w - below_w))
            total = total + ad[4, x + 1]
        quad[c] = total
        chunk = jnp.concatenate(parts, axis=0)
        send1[c] = product((cosine[0], cosine[1]), halves(chunk), NT)
        return carry

    lax.fori_loop(0, 4, block, 0)

    def scatter(source, target_ref, send_sem, recv_sem):
        def one(px, ry):
            py = peers_y[ry]
            pltpu.make_async_remote_copy(
                src_ref=source.at[:, pl.ds(px * GY + py, 1), :],
                dst_ref=target_ref.at[:, pl.ds(me, 1), :],
                send_sem=send_sem, recv_sem=recv_sem, device_id=(px, py), device_id_type=MESH,
            ).start()

        def column(rx, carry):
            px = lax.rem(gx + rx, GX)
            for ry in range(GY):
                one(px, ry)
            return carry

        lax.fori_loop(1, GX, column, 0)
        for ry in range(1, GY):
            one(gx, ry)

    def drained(source, target_ref, sem):
        count = pl.ds(0, DEV - 1)
        pltpu.make_async_copy(source.at[:, count, :], target_ref.at[:, count, :], sem).wait()

    scatter(send1, got1, s1_sem, r1_sem)
    got1[:, pl.ds(me, 1), :] = send1[:, pl.ds(me, 1), :]

    outs = [
        pltpu.make_async_copy(ad.at[pl.ds(0, 3), pl.ds(1, SX)], star, out_sem.at[0]),
        pltpu.make_async_copy(ad.at[3, pl.ds(1, SX)], theta_out, out_sem.at[1]),
        pltpu.make_async_copy(ad.at[4, pl.ds(1, SX)], vapour_out, out_sem.at[2]),
    ]
    outs[0].start()
    outs[1].start()
    fetches[1].wait()
    high, low = halves(quad[...].reshape(128, NZ))
    sums = lax.dot_general(box[...], high, (NN, ((), ())), preferred_element_type=F32)
    sums = sums + lax.dot_general(box[...], low, (NN, ((), ())), preferred_element_type=F32)
    mean = jnp.sum(sums, axis=1, keepdims=True) * (1.0 / (16 * NZ))
    soft = jnp.maximum(mean, 0.0) + jnp.log1p(jnp.exp(-jnp.abs(mean)))
    grown = radius_p + 0.5 * soft
    root = jnp.sqrt(grown)
    mass = grown * root
    gain = mass - radius_p * jnp.sqrt(radius_p)

    def other(values):
        return pltpu.roll(values, 64, 1)

    root_sum = root + other(root)
    rate = 0.05 * (root_sum * root_sum * jnp.abs(grown - other(grown)) * other(live_p))
    final = (mass + rate * other(mass)) / (1.0 + rate)
    lanes = lax.broadcasted_iota(jnp.int32, (32, 128), 1)
    own_live = jnp.where(lanes < 64, live_p, 0.0)
    cond[...] = jnp.broadcast_to(jnp.sum(own_live * gain, axis=1, keepdims=True), (32, 128)) * 0.002
    carried = [own_live, own_live * final, own_live * final * final]
    packed = jnp.zeros((32, 128), F32)
    for d in range(9):
        chosen = code_p == float(d)
        for k in range(3):
            amount = jnp.sum(jnp.where(chosen, carried[k], 0.0), axis=1, keepdims=True)
            packed = packed + jnp.where(lanes == d * 3 + k, amount, 0.0)
    load[...] = packed

    def share(source, target_ref, k, device):
        return pltpu.make_async_remote_copy(
            src_ref=source, dst_ref=target_ref, send_sem=ms_sem.at[k], recv_sem=mr_sem.at[k],
            device_id=device, device_id_type=MESH,
        )

    top, bottom = pl.ds(24, 8), pl.ds(0, 8)
    shares = [
        share(load.at[top], near.at[0, bottom], 0, (east, gy)),
        share(load.at[bottom], near.at[1, bottom], 1, (west, gy)),
        share(load, near.at[2], 2, (gx, north)),
        share(load, near.at[3], 3, (gx, south)),
        share(load.at[top], near.at[4, bottom], 4, (east, north)),
        share(load.at[top], near.at[5, bottom], 5, (east, south)),
        share(load.at[bottom], near.at[6, bottom], 6, (west, north)),
        share(load.at[bottom], near.at[7, bottom], 7, (west, south)),
    ]
    for copy in shares:
        copy.start()

    def dry(x, carry):
        first_box = (x // 4) * 8
        for t in range(4):
            drop = jnp.where(
                tile_row < 4,
                cond[pl.ds(first_box + 2 * t, 1), :],
                cond[pl.ds(first_box + 2 * t + 1, 1), :],
            )
            ad[4, x + 1, 8 * t : 8 * t + 8, :] -= drop
        return carry

    lax.fori_loop(0, SX, dry, 0)
    outs[2].start()

    for copy in fetches[2:]:
        copy.wait()
    drained(send1, got1, r1_sem)
    z_re, z_im = [], []
    for c in range(4):
        both = product((first[0, c], first[1, c]), halves(got1[c]), NN)
        z_re.append(both[:HALF])
        z_im.append(both[HALF:])

    def butterfly(re, im, sign):
        s02r, s02i = re[0] + re[2], im[0] + im[2]
        d02r, d02i = re[0] - re[2], im[0] - im[2]
        s13r, s13i = re[1] + re[3], im[1] + im[3]
        d13r, d13i = re[1] - re[3], im[1] - im[3]
        if sign < 0:
            return (
                [s02r + s13r, d02r + d13i, s02r - s13r, d02r - d13i],
                [s02i + s13i, d02i - d13r, s02i - s13i, d02i + d13r],
            )
        return (
            [s02r + s13r, d02r - d13i, s02r - s13r, d02r + d13i],
            [s02i + s13i, d02i + d13r, s02i - s13i, d02i - d13r],
        )

    q_re, q_im = butterfly(z_re, z_im, -1)
    re, im = jnp.concatenate(q_re, axis=0), jnp.concatenate(q_im, axis=0)
    turn_cos, turn_sin = turns[0], turns[1]
    joined = jnp.concatenate([re * turn_cos + im * turn_sin, im * turn_cos - re * turn_sin], axis=1)
    spectrum = product(halves(joined), (ahead[0], ahead[1]), NN)
    eigen = turns[2] + wave[pl.ds(me, 1), :]
    inverse = jnp.where(eigen == 0.0, 0.0, 1.0 / jnp.where(eigen == 0.0, 1.0, eigen))
    solved = spectrum * jnp.concatenate([inverse, inverse], axis=1)
    turned = product(halves(solved), (behind[0], behind[1]), NN)
    re, im = turned[:, :128], turned[:, 128:]
    back_re, back_im = re * turn_cos - im * turn_sin, im * turn_cos + re * turn_sin
    v_re, v_im = butterfly(
        [back_re[HALF * q : HALF * (q + 1)] for q in range(4)],
        [back_im[HALF * q : HALF * (q + 1)] for q in range(4)],
        1,
    )
    wide_lane = lax.broadcasted_iota(jnp.int32, (128, 128), 1)
    edge = None
    for c in range(4):
        stacked = jnp.concatenate([v_re[c], v_im[c]], axis=0)
        plane = product((last[0, c], last[1, c]), halves(stacked), NN)
        send2[c] = plane
        if c == 0:
            next_x = pltpu.roll(plane, 120, 0)
        picked = jnp.where((wide_lane & 31) == 0, plane, 0.0)
        picked = picked if c == 0 else pltpu.roll(picked, c, 1)
        edge = picked if edge is None else edge + picked
    row_b = lax.broadcasted_iota(jnp.int32, (128, 128), 0) & 7
    edge = jnp.where(row_b == 7, pltpu.roll(edge, 7, 0), pltpu.roll(edge, 127, 0))
    moved = pltpu.roll(edge, 36, 1)
    in_move = (wide_lane >= 36) & (wide_lane < 40)
    send2[4] = jnp.where(wide_lane < 32, next_x, jnp.where(in_move, moved, edge))

    scatter(send2, modes, s2_sem, r2_sem)
    own = pltpu.make_async_copy(
        send2.at[:, pl.ds(me, 1), :], modes.at[:, pl.ds(me, 1), :], own_sem
    )
    own.start()

    for copy in shares:
        copy.wait_recv()
    tile_lane = lax.broadcasted_iota(jnp.int32, (8, 128), 1)

    def column_of(x):
        if x < 0:
            return near[0, 0:8, :], near[4, 7:8, :], near[5, 0:1, :]
        if x > 3:
            return near[1, 0:8, :], near[6, 7:8, :], near[7, 0:1, :]
        return load[8 * x : 8 * x + 8, :], near[2, 8 * x + 7 : 8 * x + 8, :], near[3, 8 * x : 8 * x + 1, :]

    arrived = [jnp.zeros((8, 128), F32) for _ in range(4)]
    for x in range(-1, 5):
        centre, low_row, high_row = column_of(x)
        shifted = [
            jnp.where(tile_row == 7, high_row, pltpu.roll(centre, 7, 0)),
            centre,
            jnp.where(tile_row == 0, low_row, pltpu.roll(centre, 1, 0)),
        ]
        for dx in (-1, 0, 1):
            if not 0 <= x + dx < 4:
                continue
            for dy in (-1, 0, 1):
                d = (dx + 1) * 3 + dy + 1
                values = shifted[dy + 1]
                values = values if d == 0 else pltpu.roll(values, 128 - 3 * d, 1)
                arrived[x + dx] = arrived[x + dx] + values
    stacked = jnp.concatenate(arrived + [jnp.zeros((96, 128), F32)], axis=0) * (1.0 / 64)
    res[...] = stacked.T[0:8, :]
    outs.append(pltpu.make_async_copy(res, moments_out, out_sem.at[3]))
    outs[3].start()

    for copy in halo:
        copy.wait_send()
    for copy in shares:
        copy.wait_send()
    drained(send1, got1, s1_sem)
    for copy in outs:
        copy.wait()
    own.wait()
    drained(send2, send2, s2_sem)
    drained(send2, modes, r2_sem)


def final_kernel(
    modes, star, theta, vapour, moments, back_h,
    vel_out, theta_out, vapour_out, moments_out,
    mode_v, star_v, theta_v, vapour_v, mom_v, mom_o, back, pressure, in_sem, out_sem,
):
    loads = [
        pltpu.make_async_copy(source, target, in_sem.at[k])
        for k, (source, target) in enumerate(
            [(modes, mode_v), (back_h, back), (star, star_v), (theta, theta_v), (vapour, vapour_v), (moments, mom_v)]
        )
    ]
    for copy in loads:
        copy.start()
    loads[0].wait()
    loads[1].wait()
    for c in range(5):
        pressure[pl.ds(128 * c, 128), :] = product(halves(mode_v[c]), (back[0], back[1]), TN)
    for copy in loads[2:]:
        copy.wait()
    mom_o[...] = mom_v[0:3, 0:32]
    outs = [
        pltpu.make_async_copy(theta_v, theta_out, out_sem.at[0]),
        pltpu.make_async_copy(vapour_v, vapour_out, out_sem.at[1]),
        pltpu.make_async_copy(mom_o, moments_out, out_sem.at[2]),
    ]
    for copy in outs:
        copy.start()
    row = lax.broadcasted_iota(jnp.int32, (SY, NZ), 0)
    lane = lax.broadcasted_iota(jnp.int32, (SY, NZ), 1)
    for x in range(SX):
        c, i = x // 4, x % 4
        here = pressure[pl.ds(32 * x, 32), :]
        ahead = pressure[pl.ds(32 * x + 32, 32), :]
        line = 512 + (36, 32, 64, 96)[i] + c
        side = jnp.where(row == SY - 1, pressure[line : line + 1, :], pltpu.roll(here, SY - 1, 0))
        above = jnp.where(lane == NZ - 1, here, pltpu.roll(here, NZ - 1, 1))
        star_v[0, x] = star_v[0, x] - (ahead - here)
        star_v[1, x] = star_v[1, x] - (side - here)
        star_v[2, x] = star_v[2, x] - (above - here)
    last = pltpu.make_async_copy(star_v, vel_out, out_sem.at[3])
    last.start()
    for copy in outs:
        copy.wait()
    last.wait()


def shards(velocity, theta, vapour, radius_sq, multiplicity, counts, pairing, destination):
    t = tables()
    names = ["cosine", "first", "ahead", "behind", "last", "turns", "wave_z", "box"]
    held = [jnp.asarray(t[name]) for name in names]
    block = (SX, SY, NZ)
    shape = jax.ShapeDtypeStruct
    vmem = pltpu.VMEM
    dma = pltpu.SemaphoreType.DMA
    modes, star, theta_new, vapour_new, moments = pl.pallas_call(
        step_kernel,
        out_shape=(
            shape((5, DEV, 128), F32),
            shape((3,) + block, F32),
            shape(block, F32),
            shape(block, F32),
            shape((8, 128), F32),
        ),
        in_specs=[ANY] * 16,
        out_specs=(ANY,) * 5,
        scratch_shapes=[
            vmem((5, SX + 2, SY, NZ), F32),
            vmem((5, SX + 1, SY, NZ), F32),
            vmem((SY, NZ), F32),
            vmem((6, SX, NZ), F32),
            vmem((5, SX, NZ), F32),
            vmem((4, 8, NZ), F32),
            vmem((SX, NZ), F32),
            vmem((SX, NZ), F32),
            vmem((4, SY, NZ), F32),
            vmem((4, DEV, 128), F32),
            vmem((4, DEV, 128), F32),
            vmem((5, DEV, 128), F32),
        ]
        + [vmem(t[name].shape, t[name].dtype) for name in names]
        + [
            vmem((64, 32), F32),
            vmem((64, 32), F32),
            vmem((32,), jnp.int32),
            vmem((32, 64), jnp.int32),
            vmem((64, 32), jnp.int32),
            vmem((32, 128), F32),
            vmem((32, 128), F32),
            vmem((8, 32, 128), F32),
            vmem((8, 128), F32),
            dma((3,)),
            dma((5,)),
            dma((8,)),
            dma((18,)),
            dma((18,)),
            dma(()),
            dma(()),
            dma(()),
            dma(()),
            dma(()),
            dma((8,)),
            dma((8,)),
            dma((4,)),
        ],
        compiler_params=pltpu.CompilerParams(has_side_effects=True, collective_id=1),
        name="cloud_step",
    )(velocity, theta, vapour, radius_sq, multiplicity, counts, pairing, destination, *held)
    return pl.pallas_call(
        final_kernel,
        out_shape=(
            shape((3,) + block, F32),
            shape(block, F32),
            shape(block, F32),
            shape((3, 32), F32),
        ),
        in_specs=[ANY] * 6,
        out_specs=(ANY,) * 4,
        scratch_shapes=[
            vmem((5, DEV, 128), F32),
            vmem((3,) + block, F32),
            vmem(block, F32),
            vmem(block, F32),
            vmem((8, 128), F32),
            vmem((3, 32), F32),
            vmem((2, NZ, NZ), BF16),
            vmem((640, 128), F32),
            dma((6,)),
            dma((4,)),
        ],
        name="project",
    )(modes, star, theta_new, vapour_new, moments, jnp.asarray(t["back"]))


def solution(mesh):
    placed = (
        P(None, "gx", "gy", None),
        P("gx", "gy", None),
        P("gx", "gy", None),
        P(None, ("gx", "gy")),
        P(None, ("gx", "gy")),
        P(("gx", "gy")),
        P(("gx", "gy"), None),
        P(None, ("gx", "gy")),
    )
    return jax.shard_map(
        shards,
        mesh=mesh,
        in_specs=placed,
        out_specs=(
            P(None, "gx", "gy", None),
            P("gx", "gy", None),
            P("gx", "gy", None),
            P(None, ("gx", "gy")),
        ),
        check_vma=False,
    )
```

time: 107 us -> 41 us (0.38)
  Pallas kernels: 0 us -> 37.3 us
  starting transfers between devices: 27.3 us -> 0 us
  waiting for transfers between devices: 22.5 us -> 0 us
  other arithmetic: 22.4 us -> 0 us
  matrix products: 19.8 us -> 0 us
  local copies, waits for them, and re-layouts: 13.6 us -> 2.84 us
    pallas_call x0 -> x2, Pallas kernels: none -> 37.3 us  [the longest x1 34.7 us: shards(): pl.pallas_call(step_kernel, out_shape=(shape((5, DEV, 128), F32), shape((...]
    dot_general x11 -> x0, matrix products: 18 us -> none  [the longest x1 2.69 us: forward_planes(): imag_x = -jnp.einsum('kai,mabij->mkbj', sine_x, planes, precision=HIGHEST)]
    ppermute x10 -> x0, starting transfers between devices: 17.5 us -> none  [the longest x4 10.7 us: extended(): after = lax.ppermute(initial, axis, down)]
    all_to_all x2 -> x0, waiting for transfers between devices: 16.7 us -> none  [the longest x1 10.6 us: shards(): lax.all_to_all(single, ('gx', 'gy'), split_axis=2, concat_axis=1, tiled=T...]
    all_to_all x2 -> x0, starting transfers between devices: 9.77 us -> none  [the longest x1 5.38 us: shards(): lax.all_to_all(spectral, ('gx', 'gy'), split_axis=0, concat_axis=1, tiled...]
    ppermute x10 -> x0, waiting for transfers between devices: 5.79 us -> none  [the longest x4 2.77 us: extended(): after = lax.ppermute(initial, axis, down)]
    reduce_sum x7 -> x0, other arithmetic: 4.13 us -> none  [the longest x1 2.63 us: shards(): gained = jnp.sum(rate_tile * mass_grown[None, :, :], axis=1)]
    all_to_all x2 -> x0, other arithmetic: 3.35 us -> none  [the longest x1 2.05 us: shards(): lax.all_to_all(spectral, ('gx', 'gy'), split_axis=0, concat_axis=1, tiled...]
  transfers between devices with their start and end apart: 12 -> 0, of which waited for: 7 -> 0; matrix products, arithmetic and copies ran while one was open for 16% -> 0% of each run, Pallas kernels for 0% -> 0%
where the time goes in v1:
time: 41 us; the launch traced here: 40.8 us
  Pallas kernels  37.3 us (91%)
  local copies, waits for them, and re-layouts  2.84 us (7%)
  between operations  0.65 us (2%)
    pallas_call x1, Pallas kernels, shards(): pl.pallas_call(step_kernel, out_shape=(shape((5, DEV, 128), F32), shape((...  34.7 us
    unnamed x7, local copies, waits for them, and re-layouts  2.84 us
    pallas_call x1, Pallas kernels, shards(): pl.pallas_call(final_kernel, out_shape=(shape((3,) + block, F32), shape(b...  2.54 us

profile of v1, /device:TPU:1, one launch (start us, length us, event | category | flops | bytes accessed | tf_op | source)
XLA Modules:
  0.0 40.8 jit_solution(16798158325907564025)
XLA Ops:
  0.6 0.0 copy-start
  0.6 1.4 %copy.21.radius = f32[64,32]{1,0:T(8,128)} copy(f32[64,32]{0,1:T(8,128)} %param.20) | data formatting | bytes 16384 | tf_op args[3]
  2.1 0.0 copy-done
  2.1 0.0 copy-start.1
  2.1 0.7 %copy.22.multi = f32[64,32]{1,0:T(8,128)} copy(f32[64,32]{0,1:T(8,128)S(1)} %copy-done) | data formatting | bytes 16384 | tf_op args[4]
  2.8 0.0 copy-done.1
  2.8 0.7 %copy.23.dest = s32[64,32]{1,0:T(8,128)} copy(s32[64,32]{0,1:T(8,128)S(1)} %copy-done.1) | data formatting | bytes 16384 | tf_op args[7]
  3.5 34.7 %cloud_step.1 = (f32[5,128,128]{2,1,0:T(8,128)}, f32[3,16,32,128]{3,2,1,0:T(8,128)}, f32[16,32,128]{2,1,0:T(8,128)}, f32[16,32,128]{2,1,0:T(8,128)}, f32[8,128]{1,0:T(8,128)}) custom-call(f32[3,16,32,128]{3,2,1,0:T(8,128)} %vel.1, f32[16,32,128]{2,1,0:T(8,128)} %theta.1, f32[16,32,128]{2,1,0:T(8,128)} %vapour.1, f32[64,32]{1,0:T(8,128)} %copy.21.radius, ...), custom_call_target="tpu_custom_call" | custom-call | tf_op jit(solution)/shard_map/cloud_step/pallas_call | solution.py:579
  38.2 2.5 %project.1 = (f32[3,16,32,128]{3,2,1,0:T(8,128)}, f32[16,32,128]{2,1,0:T(8,128)}, f32[16,32,128]{2,1,0:T(8,128)}, f32[3,32]{1,0:T(4,128)}) custom-call(f32[5,128,128]{2,1,0:T(8,128)} %get-tuple-element.9.modes, f32[3,16,32,128]{3,2,1,0:T(8,128)} %get-tuple-element.10.star, f32[16,32,128]{2,1,0:T(8,128)} %get-tuple-element.11.theta, ...), custom_call_target="tpu_custom_call" | custom-call | tf_op jit(solution)/shard_map/project/pallas_call | solution.py:632
Async XLA Ops:
  0.6 1.4 %copy-start = (f32[64,32]{0,1:T(8,128)S(1)}, f32[64,32]{0,1:T(8,128)}, u32[]{:S(2)}) copy-start(f32[64,32]{0,1:T(8,128)} %param.21) | copy-start | bytes 24580
  2.1 0.7 %copy-start.1 = (s32[64,32]{0,1:T(8,128)S(1)}, s32[64,32]{0,1:T(8,128)}, u32[]{:S(2)}) copy-start(s32[64,32]{0,1:T(8,128)} %param.24) | copy-start | bytes 24580

commit v2 on v1

--- a/solution.py
+++ b/solution.py
@@ -17,6 +17,8 @@
 HALF = 72
 F32 = jnp.float32
 BF16 = jnp.bfloat16
+FAR_X = (10, 6, 9, 11, 14, 2, 8, 5, 7, 13, 15, 1, 3, 4, 12, 0)
+FAR_Y = (4, 3, 5, 2, 6, 1, 7, 0)
 ANY = pl.BlockSpec(memory_space=pl.ANY)
 
 
@@ -120,7 +122,7 @@
     fp, ad, xu2, yl, yh, corner, row_y0, below_y, quad, send1, got1, send2,
     cosine, first, ahead, behind, last, turns, wave, box,
     rad_v, mul_v, cnt_v, pair_v, dst_v, cond, load, near, res,
-    load_sem, drop_sem, table_sem, hs_sem, hr_sem, s1_sem, r1_sem, s2_sem, r2_sem, own_sem,
+    known, load_sem, drop_sem, table_sem, hs_sem, hr_sem, s1_sem, r1_sem, s2_sem, r2_sem, own_sem,
     ms_sem, mr_sem, out_sem,
 ):
     gx = lax.axis_index("gx")
@@ -154,42 +156,12 @@
 
     barrier = pltpu.get_barrier_semaphore()
 
-    def greet(px, ry):
-        pl.semaphore_signal(barrier, inc=1, device_id=(px, peers_y[ry]), device_id_type=MESH)
-
-    for ry in range(1, GY):
-        greet(gx, ry)
-
-    def greet_column(rx, carry):
-        px = lax.rem(gx + rx, GX)
-        for ry in range(GY):
-            greet(px, ry)
-        return carry
-
-    lax.fori_loop(1, GX, greet_column, 0)
-
-    for copy in drops:
-        copy.wait()
-    slot = lax.broadcasted_iota(jnp.int32, (64, 32), 0)
-    live = jnp.where(slot < cnt_v[...][None, :], mul_v[...], 0.0)
-    target = dst_v[...]
-    local_box = lax.broadcasted_iota(jnp.int32, (64, 32), 1)
-    source_x = gx * 4 + (local_box >> 3)
-    source_y = gy * 8 + (local_box & 7)
-    target_x = (target >> 8) * 4 + ((target & 31) >> 3)
-    target_y = ((target >> 5) & 7) * 8 + (target & 7)
-    offset_x = (target_x - source_x + 1) & 63
-    offset_y = (target_y - source_y + 1) & 63
-    code = (offset_x * 3 + offset_y).astype(F32)
-    wide = jnp.concatenate([rad_v[...], live, code, jnp.zeros((64, 32), F32)], axis=1)
-    flat = jnp.concatenate([wide, wide], axis=0).T
-    pair = pair_v[...]
-    order = jnp.concatenate([pair, pltpu.roll(jnp.concatenate([pair, pair], axis=1), 32, 1)[:, :64]], axis=1)
-    radius_p = jnp.take_along_axis(flat[0:32], order, axis=1)
-    live_p = jnp.take_along_axis(flat[32:64], order, axis=1)
-    code_p = jnp.take_along_axis(flat[64:96], order, axis=1)
-
-    pl.semaphore_wait(barrier, DEV - 1)
+    columns = (gx, east, west)
+    lines = (gy, north, south)
+    around = [(px, py) for px in columns for py in lines][1:]
+    for device in around:
+        pl.semaphore_signal(barrier, inc=1, device_id=device, device_id_type=MESH)
+    pl.semaphore_wait(barrier, len(around))
 
     def remote(source, target_ref, k, device):
         return pltpu.make_async_remote_copy(
@@ -197,28 +169,42 @@
             device_id=device, device_id_type=MESH,
         )
 
-    halo = [
+    wind = [
         remote(vel.at[:, SX - 1], fp.at[pl.ds(0, 3), 0], 0, (east, gy)),
-        remote(theta.at[SX - 1], fp.at[3, 0], 1, (east, gy)),
-        remote(vapour.at[SX - 1], fp.at[4, 0], 2, (east, gy)),
-        remote(vel.at[0, SX - 2], xu2, 3, (east, gy)),
-        remote(vel.at[:, 0], fp.at[pl.ds(0, 3), SX + 1], 4, (west, gy)),
-        remote(theta.at[0], fp.at[3, SX + 1], 5, (west, gy)),
-        remote(vapour.at[0], fp.at[4, SX + 1], 6, (west, gy)),
-        remote(vel.at[:, :, SY - 1], yl.at[pl.ds(0, 3)], 7, (gx, north)),
-        remote(theta.at[:, SY - 1], yl.at[3], 8, (gx, north)),
-        remote(vapour.at[:, SY - 1], yl.at[4], 9, (gx, north)),
-        remote(vel.at[1, :, SY - 2], yl.at[5], 10, (gx, north)),
-        remote(vel.at[:, :, 0], yh.at[pl.ds(0, 3)], 11, (gx, south)),
-        remote(theta.at[:, 0], yh.at[3], 12, (gx, south)),
-        remote(vapour.at[:, 0], yh.at[4], 13, (gx, south)),
-        remote(vel.at[0, SX - 1, pl.ds(SY - 1, 1)], corner.at[0, pl.ds(0, 1)], 14, (east, north)),
-        remote(vel.at[0, SX - 1, pl.ds(0, 1)], corner.at[1, pl.ds(0, 1)], 15, (east, south)),
-        remote(vel.at[1, SX - 1, pl.ds(SY - 1, 1)], corner.at[2, pl.ds(0, 1)], 16, (east, north)),
-        remote(vel.at[1, 0, pl.ds(SY - 1, 1)], corner.at[3, pl.ds(0, 1)], 17, (west, north)),
-    ]
+        remote(vel.at[:, 0], fp.at[pl.ds(0, 3), SX + 1], 1, (west, gy)),
+        remote(vel.at[0, SX - 2], xu2, 2, (east, gy)),
+        remote(vel.at[:, :, SY - 1], yl.at[pl.ds(0, 3)], 3, (gx, north)),
+        remote(vel.at[:, :, 0], yh.at[pl.ds(0, 3)], 4, (gx, south)),
+        remote(vel.at[1, :, SY - 2], yl.at[5], 5, (gx, north)),
+        remote(vel.at[0, SX - 1, pl.ds(SY - 1, 1)], corner.at[0, pl.ds(0, 1)], 6, (east, north)),
+        remote(vel.at[0, SX - 1, pl.ds(0, 1)], corner.at[1, pl.ds(0, 1)], 7, (east, south)),
+        remote(vel.at[1, SX - 1, pl.ds(SY - 1, 1)], corner.at[2, pl.ds(0, 1)], 8, (east, north)),
+        remote(vel.at[1, 0, pl.ds(SY - 1, 1)], corner.at[3, pl.ds(0, 1)], 9, (west, north)),
+    ]
+    air = [
+        remote(theta.at[SX - 1], fp.at[3, 0], 10, (east, gy)),
+        remote(vapour.at[SX - 1], fp.at[4, 0], 11, (east, gy)),
+        remote(theta.at[0], fp.at[3, SX + 1], 12, (west, gy)),
+        remote(vapour.at[0], fp.at[4, SX + 1], 13, (west, gy)),
+        remote(theta.at[:, SY - 1], yl.at[3], 14, (gx, north)),
+        remote(vapour.at[:, SY - 1], yl.at[4], 15, (gx, north)),
+        remote(theta.at[:, 0], yh.at[3], 16, (gx, south)),
+        remote(vapour.at[:, 0], yh.at[4], 17, (gx, south)),
+    ]
+    halo = wind + air
     for copy in halo:
         copy.start()
+
+    def pass_on(k, devices):
+        for device in devices:
+            pl.semaphore_signal(known.at[k], inc=1, device_id=device, device_id_type=MESH)
+
+    def away(step_x, step_y):
+        return lax.rem(gx + GX + step_x, GX), lax.rem(gy + GY + step_y, GY)
+
+    second = [away(i, j) for i in (-2, 0, 2) for j in (-2, 0, 2) if i or j]
+    third = [away(-4, 0), away(4, 0)]
+    pass_on(0, around)
     for copy in loads:
         copy.wait()
 
@@ -242,30 +228,36 @@
         centre = 0.94 + jnp.where(top, up, 0.0) + jnp.where(bottom, down, 0.0)
         return jnp.where(top, 0.0, up), jnp.where(bottom, 0.0, down), centre
 
-    def advect_plane(x):
+    def advect_plane(x, fields):
         c_east, c_west = coefficients(fp[0, x + 1])
         c_north, c_south = coefficients(fp[1, x + 1])
         c_north = jnp.where(row == SY - 1, 0.0, c_north)
         c_south = jnp.where(row == 0, 0.0, c_south)
         c_up, c_down, c_mid = vertical(fp[2, x + 1], lane)
-        for f in range(5):
+        for f in fields:
             centre = fp[f, x + 1]
             ad[f, x + 1] = (
                 (c_mid * centre + c_east * fp[f, x + 2] + c_west * fp[f, x])
                 + (c_north * pltpu.roll(centre, SY - 1, 0) + c_south * pltpu.roll(centre, 1, 0))
                 + (c_up * upward(centre) + c_down * downward(centre))
             )
+
+    def inner(x, carry):
+        advect_plane(x, (0, 1, 2))
         row_y0[pl.ds(x, 1), :] = fp[1, x + 1, 0:1, :]
-
-    def inner(x, carry):
-        advect_plane(x)
         return carry
 
     lax.fori_loop(1, SX - 1, inner, 0)
-    for copy in halo:
+    pl.semaphore_wait(known.at[0], len(around))
+    pass_on(1, second)
+    for x in (0, SX - 1):
+        row_y0[pl.ds(x, 1), :] = fp[1, x + 1, 0:1, :]
+    for copy in wind:
         copy.wait_recv()
-    advect_plane(0)
-    advect_plane(SX - 1)
+    pl.semaphore_wait(known.at[1], len(second))
+    pass_on(2, third)
+    advect_plane(0, (0, 1, 2))
+    advect_plane(SX - 1, (0, 1, 2))
 
     speed = fp[0, 0]
     c_east, c_west = coefficients(speed)
@@ -293,31 +285,42 @@
     )
     fetches[0].wait()
 
+    def border(x, fields):
+        _, c_south = coefficients(fp[1, x + 1, 0:8, :])
+        c_north, _ = coefficients(fp[1, x + 1, SY - 8 : SY, :])
+        c_south = jnp.where(tile_row == 0, c_south, 0.0)
+        c_north = jnp.where(tile_row == 7, c_north, 0.0)
+        for f in fields:
+            ad[f, x + 1, 0:8, :] += c_south * yl[f, pl.ds(x, 1), :]
+            ad[f, x + 1, SY - 8 : SY, :] += c_north * yh[f, pl.ds(x, 1), :]
+
     def block(c, carry):
-        total = jnp.zeros((SY, NZ), F32)
         parts = []
         for i in range(4):
             x = c * 4 + i
-            _, c_south = coefficients(fp[1, x + 1, 0:8, :])
-            c_north, _ = coefficients(fp[1, x + 1, SY - 8 : SY, :])
-            c_south = jnp.where(tile_row == 0, c_south, 0.0)
-            c_north = jnp.where(tile_row == 7, c_north, 0.0)
-            for f in range(5):
-                ad[f, x + 1, 0:8, :] += c_south * yl[f, pl.ds(x, 1), :]
-                ad[f, x + 1, SY - 8 : SY, :] += c_north * yh[f, pl.ds(x, 1), :]
+            border(x, (0, 1, 2))
             star_w = ad[2, x + 1] + 0.1 * fp[3, x + 1]
             ad[2, x + 1] = star_w
             star_v = ad[1, x + 1]
             behind_v = jnp.where(row == 0, below_y[pl.ds(x, 1), :], pltpu.roll(star_v, 1, 0))
             below_w = jnp.where(lane == 0, 0.0, downward(star_w))
             parts.append((ad[0, x + 1] - ad[0, x]) + (star_v - behind_v) + (star_w - below_w))
-            total = total + ad[4, x + 1]
-        quad[c] = total
         chunk = jnp.concatenate(parts, axis=0)
         send1[c] = product((cosine[0], cosine[1]), halves(chunk), NT)
         return carry
 
+    def scalars(c, carry):
+        total = jnp.zeros((SY, NZ), F32)
+        for i in range(4):
+            x = c * 4 + i
+            advect_plane(x, (3, 4))
+            border(x, (3, 4))
+            total = total + ad[4, x + 1]
+        quad[c] = total
+        return carry
+
     lax.fori_loop(0, 4, block, 0)
+    pl.semaphore_wait(known.at[2], len(third))
 
     def scatter(source, target_ref, send_sem, recv_sem):
         def one(px, ry):
@@ -328,15 +331,11 @@
                 send_sem=send_sem, recv_sem=recv_sem, device_id=(px, py), device_id_type=MESH,
             ).start()
 
-        def column(rx, carry):
+        for rx in FAR_X:
             px = lax.rem(gx + rx, GX)
-            for ry in range(GY):
-                one(px, ry)
-            return carry
-
-        lax.fori_loop(1, GX, column, 0)
-        for ry in range(1, GY):
-            one(gx, ry)
+            for ry in FAR_Y:
+                if rx or ry:
+                    one(px, ry)
 
     def drained(source, target_ref, sem):
         count = pl.ds(0, DEV - 1)
@@ -351,6 +350,36 @@
         pltpu.make_async_copy(ad.at[4, pl.ds(1, SX)], vapour_out, out_sem.at[2]),
     ]
     outs[0].start()
+    for copy in drops:
+        copy.wait()
+    box_row = lax.broadcasted_iota(jnp.int32, (32, 32), 0)
+    box_lane = lax.broadcasted_iota(jnp.int32, (32, 32), 1)
+    spread = jnp.where(box_row == box_lane, cnt_v[...][None, :].astype(F32), 0.0)
+    used = jnp.sum(spread, axis=1, keepdims=True)
+    slot = lax.broadcasted_iota(jnp.int32, (32, 64), 1).astype(F32)
+    live = jnp.where(slot < used, mul_v[...], 0.0)
+    target = dst_v[...]
+    local_box = lax.broadcasted_iota(jnp.int32, (32, 64), 0)
+    source_x = gx * 4 + (local_box >> 3)
+    source_y = gy * 8 + (local_box & 7)
+    target_x = (target >> 8) * 4 + ((target & 31) >> 3)
+    target_y = ((target >> 5) & 7) * 8 + (target & 7)
+    offset_x = (target_x - source_x + 1) & 63
+    offset_y = (target_y - source_y + 1) & 63
+    code = (offset_x * 3 + offset_y).astype(F32)
+
+    def twice(values):
+        return jnp.concatenate([values, values], axis=1)
+
+    pair = twice(pair_v[...])
+    order = jnp.where(lax.broadcasted_iota(jnp.int32, (32, 128), 1) < 64, pair, pltpu.roll(pair, 32, 1))
+    radius_p = jnp.take_along_axis(twice(rad_v[...]), order, axis=1)
+    live_p = jnp.take_along_axis(twice(live), order, axis=1)
+    code_p = jnp.take_along_axis(twice(code), order, axis=1)
+
+    for copy in air:
+        copy.wait_recv()
+    lax.fori_loop(0, 4, scalars, 0)
     outs[1].start()
     fetches[1].wait()
     high, low = halves(quad[...].reshape(128, NZ))
@@ -603,15 +632,16 @@
         ]
         + [vmem(t[name].shape, t[name].dtype) for name in names]
         + [
-            vmem((64, 32), F32),
-            vmem((64, 32), F32),
+            vmem((32, 64), F32),
+            vmem((32, 64), F32),
             vmem((32,), jnp.int32),
             vmem((32, 64), jnp.int32),
-            vmem((64, 32), jnp.int32),
+            vmem((32, 64), jnp.int32),
             vmem((32, 128), F32),
             vmem((32, 128), F32),
             vmem((8, 32, 128), F32),
             vmem((8, 128), F32),
+            pltpu.SemaphoreType.REGULAR((3,)),
             dma((3,)),
             dma((5,)),
             dma((8,)),
@@ -628,7 +658,7 @@
         ],
         compiler_params=pltpu.CompilerParams(has_side_effects=True, collective_id=1),
         name="cloud_step",
-    )(velocity, theta, vapour, radius_sq, multiplicity, counts, pairing, destination, *held)
+    )(velocity, theta, vapour, radius_sq.T, multiplicity.T, counts, pairing, destination.T, *held)
     return pl.pallas_call(
         final_kernel,
         out_shape=(

time: 41 us -> 37.2 us (0.907)
  local copies, waits for them, and re-layouts: 2.84 us -> 0 us
  Pallas kernels: 37.3 us -> 36.4 us
    unnamed x7 -> x0, local copies, waits for them, and re-layouts: 2.84 us -> none
    pallas_call x1, Pallas kernels: 34.7 us -> 33.9 us  [shards(): pl.pallas_call(step_kernel, out_shape=(shape((5, DEV, 128), F32), shape((...]
where the time goes in v2:
time: 37.2 us; the launch traced here: 37.1 us
  Pallas kernels  36.4 us (98%)
  between operations  0.64 us (2%)
    pallas_call x1, Pallas kernels, shards(): pl.pallas_call(step_kernel, out_shape=(shape((5, DEV, 128), F32), shape((...  33.9 us
    pallas_call x1, Pallas kernels, shards(): pl.pallas_call(final_kernel, out_shape=(shape((3,) + block, F32), shape(b...  2.54 us

profile of v2, /device:TPU:1, one launch (start us, length us, event | category | flops | bytes accessed | tf_op | source)
XLA Modules:
  0.0 37.1 jit_solution(10107781681238466875)
XLA Ops:
  0.6 33.9 %cloud_step.1 = (f32[5,128,128]{2,1,0:T(8,128)}, f32[3,16,32,128]{3,2,1,0:T(8,128)}, f32[16,32,128]{2,1,0:T(8,128)}, f32[16,32,128]{2,1,0:T(8,128)}, f32[8,128]{1,0:T(8,128)}) custom-call(f32[3,16,32,128]{3,2,1,0:T(8,128)} %vel.1, f32[16,32,128]{2,1,0:T(8,128)} %theta.1, f32[16,32,128]{2,1,0:T(8,128)} %vapour.1, f32[32,64]{1,0:T(8,128)} %bitcast.3, ...), custom_call_target="tpu_custom_call" | custom-call | tf_op jit(solution)/shard_map/cloud_step/pallas_call | solution.py:608
  34.5 2.5 %project.1 = (f32[3,16,32,128]{3,2,1,0:T(8,128)}, f32[16,32,128]{2,1,0:T(8,128)}, f32[16,32,128]{2,1,0:T(8,128)}, f32[3,32]{1,0:T(4,128)}) custom-call(f32[5,128,128]{2,1,0:T(8,128)} %get-tuple-element.9.modes, f32[3,16,32,128]{3,2,1,0:T(8,128)} %get-tuple-element.10.star, f32[16,32,128]{2,1,0:T(8,128)} %get-tuple-element.11.theta, ...), custom_call_target="tpu_custom_call" | custom-call | tf_op jit(solution)/shard_map/project/pallas_call | solution.py:662

commit v3 on v2

--- a/solution.py
+++ b/solution.py
@@ -17,8 +17,6 @@
 HALF = 72
 F32 = jnp.float32
 BF16 = jnp.bfloat16
-FAR_X = (10, 6, 9, 11, 14, 2, 8, 5, 7, 13, 15, 1, 3, 4, 12, 0)
-FAR_Y = (4, 3, 5, 2, 6, 1, 7, 0)
 ANY = pl.BlockSpec(memory_space=pl.ANY)
 
 
@@ -27,6 +25,23 @@
     high = table.astype(jnp.bfloat16)
     low = (table - high.astype(np.float32)).astype(jnp.bfloat16)
     return np.stack([high, low])
+
+
+@functools.cache
+def send_order():
+    hops = (0, 1, 2, 1)
+    peers = [(rx, ry) for rx in range(GX) for ry in range(GY) if rx or ry]
+    peers.sort(key=lambda p: -(hops[p[0] // 4] + hops[p[0] % 4] + hops[p[1] // 2]))
+    classes = {}
+    for p in peers:
+        classes.setdefault((p[0] // 4 > 2, p[0] % 4 > 2, p[1] // 2 > 2, p[1] % 2), []).append(p)
+    queues = list(classes.values())
+    order = []
+    while any(queues):
+        for queue in queues:
+            if queue:
+                order.append(queue.pop(0))
+    return tuple(order)
 
 
 @functools.cache
@@ -130,6 +145,7 @@
     me = gx * GY + gy
     east, west = lax.rem(gx + 1, GX), lax.rem(gx + GX - 1, GX)
     north, south = lax.rem(gy + 1, GY), lax.rem(gy + GY - 1, GY)
+    peers_x = [lax.rem(gx + r, GX) for r in range(GX)]
     peers_y = [lax.rem(gy + r, GY) for r in range(GY)]
 
     loads = [
@@ -156,9 +172,18 @@
 
     barrier = pltpu.get_barrier_semaphore()
 
-    columns = (gx, east, west)
-    lines = (gy, north, south)
-    around = [(px, py) for px in columns for py in lines][1:]
+    chip_z, chip_x, chip_y, core = gx // 4, lax.rem(gx, 4), gy // 2, lax.rem(gy, 2)
+
+    def away(step_z, step_x, step_y, step_core):
+        to_z, to_x, to_y = (
+            lax.rem(at + 4 + step, 4)
+            for at, step in ((chip_z, step_z), (chip_x, step_x), (chip_y, step_y))
+        )
+        return to_z * 4 + to_x, to_y * 2 + lax.rem(core + step_core, 2)
+
+    steps = [(k, i, j, n) for k in (0, 1, -1) for i in (1, -1, 0) for j in (1, -1, 0) for n in (0, 1)]
+    around = [away(*step) for step in steps if any(step)]
+    corners = [away(k, i, j, 0) for k in (1, -1) for i in (1, -1) for j in (1, -1)]
     for device in around:
         pl.semaphore_signal(barrier, inc=1, device_id=device, device_id_type=MESH)
     pl.semaphore_wait(barrier, len(around))
@@ -192,19 +217,14 @@
         remote(vapour.at[:, 0], yh.at[4], 17, (gx, south)),
     ]
     halo = wind + air
-    for copy in halo:
+    for copy in wind[6:] + wind[:6]:
         copy.start()
 
     def pass_on(k, devices):
         for device in devices:
             pl.semaphore_signal(known.at[k], inc=1, device_id=device, device_id_type=MESH)
 
-    def away(step_x, step_y):
-        return lax.rem(gx + GX + step_x, GX), lax.rem(gy + GY + step_y, GY)
-
-    second = [away(i, j) for i in (-2, 0, 2) for j in (-2, 0, 2) if i or j]
-    third = [away(-4, 0), away(4, 0)]
-    pass_on(0, around)
+    pass_on(0, corners)
     for copy in loads:
         copy.wait()
 
@@ -248,14 +268,39 @@
         return carry
 
     lax.fori_loop(1, SX - 1, inner, 0)
-    pl.semaphore_wait(known.at[0], len(around))
-    pass_on(1, second)
+    for copy in drops:
+        copy.wait()
+    box_row = lax.broadcasted_iota(jnp.int32, (32, 32), 0)
+    box_lane = lax.broadcasted_iota(jnp.int32, (32, 32), 1)
+    spread = jnp.where(box_row == box_lane, cnt_v[...][None, :].astype(F32), 0.0)
+    used = jnp.sum(spread, axis=1, keepdims=True)
+    slot = lax.broadcasted_iota(jnp.int32, (32, 64), 1).astype(F32)
+    live = jnp.where(slot < used, mul_v[...], 0.0)
+    target = dst_v[...]
+    local_box = lax.broadcasted_iota(jnp.int32, (32, 64), 0)
+    source_x = gx * 4 + (local_box >> 3)
+    source_y = gy * 8 + (local_box & 7)
+    target_x = (target >> 8) * 4 + ((target & 31) >> 3)
+    target_y = ((target >> 5) & 7) * 8 + (target & 7)
+    offset_x = (target_x - source_x + 1) & 63
+    offset_y = (target_y - source_y + 1) & 63
+    code = (offset_x * 3 + offset_y).astype(F32)
+
+    def twice(values):
+        return jnp.concatenate([values, values], axis=1)
+
+    pair = twice(pair_v[...])
+    order = jnp.where(lax.broadcasted_iota(jnp.int32, (32, 128), 1) < 64, pair, pltpu.roll(pair, 32, 1))
+    radius_p = jnp.take_along_axis(twice(rad_v[...]), order, axis=1)
+    live_p = jnp.take_along_axis(twice(live), order, axis=1)
+    code_p = jnp.take_along_axis(twice(code), order, axis=1)
+
     for x in (0, SX - 1):
         row_y0[pl.ds(x, 1), :] = fp[1, x + 1, 0:1, :]
     for copy in wind:
         copy.wait_recv()
-    pl.semaphore_wait(known.at[1], len(second))
-    pass_on(2, third)
+    for copy in air:
+        copy.start()
     advect_plane(0, (0, 1, 2))
     advect_plane(SX - 1, (0, 1, 2))
 
@@ -320,7 +365,7 @@
         return carry
 
     lax.fori_loop(0, 4, block, 0)
-    pl.semaphore_wait(known.at[2], len(third))
+    pl.semaphore_wait(known.at[0], len(corners))
 
     def scatter(source, target_ref, send_sem, recv_sem):
         def one(px, ry):
@@ -331,11 +376,8 @@
                 send_sem=send_sem, recv_sem=recv_sem, device_id=(px, py), device_id_type=MESH,
             ).start()
 
-        for rx in FAR_X:
-            px = lax.rem(gx + rx, GX)
-            for ry in FAR_Y:
-                if rx or ry:
-                    one(px, ry)
+        for rx, ry in send_order():
+            one(peers_x[rx], ry)
 
     def drained(source, target_ref, sem):
         count = pl.ds(0, DEV - 1)
@@ -350,33 +392,6 @@
         pltpu.make_async_copy(ad.at[4, pl.ds(1, SX)], vapour_out, out_sem.at[2]),
     ]
     outs[0].start()
-    for copy in drops:
-        copy.wait()
-    box_row = lax.broadcasted_iota(jnp.int32, (32, 32), 0)
-    box_lane = lax.broadcasted_iota(jnp.int32, (32, 32), 1)
-    spread = jnp.where(box_row == box_lane, cnt_v[...][None, :].astype(F32), 0.0)
-    used = jnp.sum(spread, axis=1, keepdims=True)
-    slot = lax.broadcasted_iota(jnp.int32, (32, 64), 1).astype(F32)
-    live = jnp.where(slot < used, mul_v[...], 0.0)
-    target = dst_v[...]
-    local_box = lax.broadcasted_iota(jnp.int32, (32, 64), 0)
-    source_x = gx * 4 + (local_box >> 3)
-    source_y = gy * 8 + (local_box & 7)
-    target_x = (target >> 8) * 4 + ((target & 31) >> 3)
-    target_y = ((target >> 5) & 7) * 8 + (target & 7)
-    offset_x = (target_x - source_x + 1) & 63
-    offset_y = (target_y - source_y + 1) & 63
-    code = (offset_x * 3 + offset_y).astype(F32)
-
-    def twice(values):
-        return jnp.concatenate([values, values], axis=1)
-
-    pair = twice(pair_v[...])
-    order = jnp.where(lax.broadcasted_iota(jnp.int32, (32, 128), 1) < 64, pair, pltpu.roll(pair, 32, 1))
-    radius_p = jnp.take_along_axis(twice(rad_v[...]), order, axis=1)
-    live_p = jnp.take_along_axis(twice(live), order, axis=1)
-    code_p = jnp.take_along_axis(twice(code), order, axis=1)
-
     for copy in air:
         copy.wait_recv()
     lax.fori_loop(0, 4, scalars, 0)
@@ -641,7 +656,7 @@
             vmem((32, 128), F32),
             vmem((8, 32, 128), F32),
             vmem((8, 128), F32),
-            pltpu.SemaphoreType.REGULAR((3,)),
+            pltpu.SemaphoreType.REGULAR((1,)),
             dma((3,)),
             dma((5,)),
             dma((8,)),

time: 37.2 us -> 35.4 us (0.952)
  Pallas kernels: 36.4 us -> 34.6 us
    pallas_call x1, Pallas kernels: 33.9 us -> 32.1 us  [shards(): pl.pallas_call(step_kernel, out_shape=(shape((5, DEV, 128), F32), shape((...]
where the time goes in v3:
time: 35.4 us; the launch traced here: 35.2 us
  Pallas kernels  34.6 us (98%)
  between operations  0.64 us (2%)
    pallas_call x1, Pallas kernels, shards(): pl.pallas_call(step_kernel, out_shape=(shape((5, DEV, 128), F32), shape((...  32.1 us
    pallas_call x1, Pallas kernels, shards(): pl.pallas_call(final_kernel, out_shape=(shape((3,) + block, F32), shape(b...  2.54 us

profile of v3, /device:TPU:1, one launch (start us, length us, event | category | flops | bytes accessed | tf_op | source)
XLA Modules:
  0.0 35.2 jit_solution(12398728994906461635)
XLA Ops:
  0.6 32.1 %cloud_step.1 = (f32[5,128,128]{2,1,0:T(8,128)}, f32[3,16,32,128]{3,2,1,0:T(8,128)}, f32[16,32,128]{2,1,0:T(8,128)}, f32[16,32,128]{2,1,0:T(8,128)}, f32[8,128]{1,0:T(8,128)}) custom-call(f32[3,16,32,128]{3,2,1,0:T(8,128)} %vel.1, f32[16,32,128]{2,1,0:T(8,128)} %theta.1, f32[16,32,128]{2,1,0:T(8,128)} %vapour.1, f32[32,64]{1,0:T(8,128)} %bitcast.3, ...), custom_call_target="tpu_custom_call" | custom-call | tf_op jit(solution)/shard_map/cloud_step/pallas_call | solution.py:623
  32.7 2.5 %project.1 = (f32[3,16,32,128]{3,2,1,0:T(8,128)}, f32[16,32,128]{2,1,0:T(8,128)}, f32[16,32,128]{2,1,0:T(8,128)}, f32[3,32]{1,0:T(4,128)}) custom-call(f32[5,128,128]{2,1,0:T(8,128)} %get-tuple-element.9.modes, f32[3,16,32,128]{3,2,1,0:T(8,128)} %get-tuple-element.10.star, f32[16,32,128]{2,1,0:T(8,128)} %get-tuple-element.11.theta, ...), custom_call_target="tpu_custom_call" | custom-call | tf_op jit(solution)/shard_map/project/pallas_call | solution.py:677

commit v4 on v3

--- a/solution.py
+++ b/solution.py
@@ -133,12 +133,12 @@
 def step_kernel(
     vel, theta, vapour, radius, multi, counts, pairing, dest,
     cosine_h, first_h, ahead_h, behind_h, last_h, turns_h, wave_h, box_h,
-    modes, star, theta_out, vapour_out, moments_out,
-    fp, ad, xu2, yl, yh, corner, row_y0, below_y, quad, send1, got1, send2,
+    modes, ad, moments_out,
+    fp, before_u, xu2, yl, yh, corner, row_y0, below_y, quad, send1, got1, send2,
     cosine, first, ahead, behind, last, turns, wave, box,
-    rad_v, mul_v, cnt_v, pair_v, dst_v, cond, load, near, res,
-    known, load_sem, drop_sem, table_sem, hs_sem, hr_sem, s1_sem, r1_sem, s2_sem, r2_sem, own_sem,
-    ms_sem, mr_sem, out_sem,
+    rad_v, mul_v, cnt_v, pair_v, dst_v, cond, load, near,
+    known, load_sem, drop_sem, table_sem, hs_sem, hr_sem, s1_sem, r1_sem, s2_sem, r2_sem,
+    ms_sem, mr_sem,
 ):
     gx = lax.axis_index("gx")
     gy = lax.axis_index("gy")
@@ -256,7 +256,7 @@
         c_up, c_down, c_mid = vertical(fp[2, x + 1], lane)
         for f in fields:
             centre = fp[f, x + 1]
-            ad[f, x + 1] = (
+            ad[f, x] = (
                 (c_mid * centre + c_east * fp[f, x + 2] + c_west * fp[f, x])
                 + (c_north * pltpu.roll(centre, SY - 1, 0) + c_south * pltpu.roll(centre, 1, 0))
                 + (c_up * upward(centre) + c_down * downward(centre))
@@ -310,7 +310,7 @@
     c_up, c_down, c_mid = vertical(fp[2, 0], lane)
     above = jnp.where(row == SY - 1, corner[1, 0:1, :], pltpu.roll(speed, SY - 1, 0))
     beneath = jnp.where(row == 0, corner[0, 0:1, :], pltpu.roll(speed, 1, 0))
-    ad[0, 0] = (
+    before_u[...] = (
         (c_mid * speed + c_east * fp[0, 1] + c_west * xu2[...])
         + (c_north * above + c_south * beneath)
         + (c_up * upward(speed) + c_down * downward(speed))
@@ -336,20 +336,24 @@
         c_south = jnp.where(tile_row == 0, c_south, 0.0)
         c_north = jnp.where(tile_row == 7, c_north, 0.0)
         for f in fields:
-            ad[f, x + 1, 0:8, :] += c_south * yl[f, pl.ds(x, 1), :]
-            ad[f, x + 1, SY - 8 : SY, :] += c_north * yh[f, pl.ds(x, 1), :]
+            ad[f, x, 0:8, :] += c_south * yl[f, pl.ds(x, 1), :]
+            ad[f, x, SY - 8 : SY, :] += c_north * yh[f, pl.ds(x, 1), :]
 
     def block(c, carry):
         parts = []
         for i in range(4):
             x = c * 4 + i
             border(x, (0, 1, 2))
-            star_w = ad[2, x + 1] + 0.1 * fp[3, x + 1]
-            ad[2, x + 1] = star_w
-            star_v = ad[1, x + 1]
+            star_w = ad[2, x] + 0.1 * fp[3, x + 1]
+            ad[2, x] = star_w
+            star_v = ad[1, x]
+            star_u = ad[0, x]
+            if i == 0:
+                last_u = jnp.where(c == 0, before_u[...], ad[0, jnp.maximum(x - 1, 0)])
             behind_v = jnp.where(row == 0, below_y[pl.ds(x, 1), :], pltpu.roll(star_v, 1, 0))
             below_w = jnp.where(lane == 0, 0.0, downward(star_w))
-            parts.append((ad[0, x + 1] - ad[0, x]) + (star_v - behind_v) + (star_w - below_w))
+            parts.append((star_u - last_u) + (star_v - behind_v) + (star_w - below_w))
+            last_u = star_u
         chunk = jnp.concatenate(parts, axis=0)
         send1[c] = product((cosine[0], cosine[1]), halves(chunk), NT)
         return carry
@@ -360,7 +364,7 @@
             x = c * 4 + i
             advect_plane(x, (3, 4))
             border(x, (3, 4))
-            total = total + ad[4, x + 1]
+            total = total + ad[4, x]
         quad[c] = total
         return carry
 
@@ -386,16 +390,9 @@
     scatter(send1, got1, s1_sem, r1_sem)
     got1[:, pl.ds(me, 1), :] = send1[:, pl.ds(me, 1), :]
 
-    outs = [
-        pltpu.make_async_copy(ad.at[pl.ds(0, 3), pl.ds(1, SX)], star, out_sem.at[0]),
-        pltpu.make_async_copy(ad.at[3, pl.ds(1, SX)], theta_out, out_sem.at[1]),
-        pltpu.make_async_copy(ad.at[4, pl.ds(1, SX)], vapour_out, out_sem.at[2]),
-    ]
-    outs[0].start()
     for copy in air:
         copy.wait_recv()
     lax.fori_loop(0, 4, scalars, 0)
-    outs[1].start()
     fetches[1].wait()
     high, low = halves(quad[...].reshape(128, NZ))
     sums = lax.dot_general(box[...], high, (NN, ((), ())), preferred_element_type=F32)
@@ -453,11 +450,10 @@
                 cond[pl.ds(first_box + 2 * t, 1), :],
                 cond[pl.ds(first_box + 2 * t + 1, 1), :],
             )
-            ad[4, x + 1, 8 * t : 8 * t + 8, :] -= drop
+            ad[4, x, 8 * t : 8 * t + 8, :] -= drop
         return carry
 
     lax.fori_loop(0, SX, dry, 0)
-    outs[2].start()
 
     for copy in fetches[2:]:
         copy.wait()
@@ -517,10 +513,7 @@
     send2[4] = jnp.where(wide_lane < 32, next_x, jnp.where(in_move, moved, edge))
 
     scatter(send2, modes, s2_sem, r2_sem)
-    own = pltpu.make_async_copy(
-        send2.at[:, pl.ds(me, 1), :], modes.at[:, pl.ds(me, 1), :], own_sem
-    )
-    own.start()
+    modes[:, pl.ds(me, 1), :] = send2[:, pl.ds(me, 1), :]
 
     for copy in shares:
         copy.wait_recv()
@@ -550,66 +543,55 @@
                 values = values if d == 0 else pltpu.roll(values, 128 - 3 * d, 1)
                 arrived[x + dx] = arrived[x + dx] + values
     stacked = jnp.concatenate(arrived + [jnp.zeros((96, 128), F32)], axis=0) * (1.0 / 64)
-    res[...] = stacked.T[0:8, :]
-    outs.append(pltpu.make_async_copy(res, moments_out, out_sem.at[3]))
-    outs[3].start()
+    moments_out[...] = stacked.T[0:8, :]
 
     for copy in halo:
         copy.wait_send()
     for copy in shares:
         copy.wait_send()
     drained(send1, got1, s1_sem)
-    for copy in outs:
-        copy.wait()
-    own.wait()
     drained(send2, send2, s2_sem)
     drained(send2, modes, r2_sem)
 
 
 def final_kernel(
-    modes, star, theta, vapour, moments, back_h,
+    modes, ad, moments, back,
     vel_out, theta_out, vapour_out, moments_out,
-    mode_v, star_v, theta_v, vapour_v, mom_v, mom_o, back, pressure, in_sem, out_sem,
+    fresh, mom_o, pressure, out_sem,
 ):
-    loads = [
-        pltpu.make_async_copy(source, target, in_sem.at[k])
-        for k, (source, target) in enumerate(
-            [(modes, mode_v), (back_h, back), (star, star_v), (theta, theta_v), (vapour, vapour_v), (moments, mom_v)]
-        )
-    ]
-    for copy in loads:
-        copy.start()
-    loads[0].wait()
-    loads[1].wait()
-    for c in range(5):
-        pressure[pl.ds(128 * c, 128), :] = product(halves(mode_v[c]), (back[0], back[1]), TN)
-    for copy in loads[2:]:
-        copy.wait()
-    mom_o[...] = mom_v[0:3, 0:32]
+    mom_o[...] = moments[0:3, 0:32]
     outs = [
-        pltpu.make_async_copy(theta_v, theta_out, out_sem.at[0]),
-        pltpu.make_async_copy(vapour_v, vapour_out, out_sem.at[1]),
+        pltpu.make_async_copy(ad.at[3], theta_out, out_sem.at[0]),
+        pltpu.make_async_copy(ad.at[4], vapour_out, out_sem.at[1]),
         pltpu.make_async_copy(mom_o, moments_out, out_sem.at[2]),
     ]
     for copy in outs:
         copy.start()
     row = lax.broadcasted_iota(jnp.int32, (SY, NZ), 0)
     lane = lax.broadcasted_iota(jnp.int32, (SY, NZ), 1)
-    for x in range(SX):
-        c, i = x // 4, x % 4
-        here = pressure[pl.ds(32 * x, 32), :]
-        ahead = pressure[pl.ds(32 * x + 32, 32), :]
-        line = 512 + (36, 32, 64, 96)[i] + c
-        side = jnp.where(row == SY - 1, pressure[line : line + 1, :], pltpu.roll(here, SY - 1, 0))
-        above = jnp.where(lane == NZ - 1, here, pltpu.roll(here, NZ - 1, 1))
-        star_v[0, x] = star_v[0, x] - (ahead - here)
-        star_v[1, x] = star_v[1, x] - (side - here)
-        star_v[2, x] = star_v[2, x] - (above - here)
-    last = pltpu.make_async_copy(star_v, vel_out, out_sem.at[3])
-    last.start()
+
+    def levels(c):
+        pressure[pl.ds(128 * c, 128), :] = product(halves(modes[c]), (back[0], back[1]), TN)
+
+    levels(4)
+    for c in (3, 2, 1, 0):
+        levels(c)
+        for i in range(4):
+            x = 4 * c + i
+            here = pressure[pl.ds(32 * x, 32), :]
+            ahead = pressure[pl.ds(32 * x + 32, 32), :]
+            line = 512 + (36, 32, 64, 96)[i] + c
+            side = jnp.where(row == SY - 1, pressure[line : line + 1, :], pltpu.roll(here, SY - 1, 0))
+            above = jnp.where(lane == NZ - 1, here, pltpu.roll(here, NZ - 1, 1))
+            fresh[0, x] = ad[0, x] - (ahead - here)
+            fresh[1, x] = ad[1, x] - (side - here)
+            fresh[2, x] = ad[2, x] - (above - here)
+        part = pl.ds(4 * c, 4)
+        copy = pltpu.make_async_copy(fresh.at[:, part], vel_out.at[:, part], out_sem.at[3 + c])
+        copy.start()
+        outs.append(copy)
     for copy in outs:
         copy.wait()
-    last.wait()
 
 
 def shards(velocity, theta, vapour, radius_sq, multiplicity, counts, pairing, destination):
@@ -620,20 +602,19 @@
     shape = jax.ShapeDtypeStruct
     vmem = pltpu.VMEM
     dma = pltpu.SemaphoreType.DMA
-    modes, star, theta_new, vapour_new, moments = pl.pallas_call(
+    here = pl.BlockSpec(memory_space=pltpu.VMEM)
+    modes, advected, moments = pl.pallas_call(
         step_kernel,
         out_shape=(
-            shape((5, DEV, 128), F32),
-            shape((3,) + block, F32),
-            shape(block, F32),
-            shape(block, F32),
-            shape((8, 128), F32),
+            vmem((5, DEV, 128), F32),
+            vmem((5,) + block, F32),
+            vmem((8, 128), F32),
         ),
         in_specs=[ANY] * 16,
-        out_specs=(ANY,) * 5,
+        out_specs=(here,) * 3,
         scratch_shapes=[
             vmem((5, SX + 2, SY, NZ), F32),
-            vmem((5, SX + 1, SY, NZ), F32),
+            vmem((SY, NZ), F32),
             vmem((SY, NZ), F32),
             vmem((6, SX, NZ), F32),
             vmem((5, SX, NZ), F32),
@@ -655,7 +636,6 @@
             vmem((32, 128), F32),
             vmem((32, 128), F32),
             vmem((8, 32, 128), F32),
-            vmem((8, 128), F32),
             pltpu.SemaphoreType.REGULAR((1,)),
             dma((3,)),
             dma((5,)),
@@ -666,14 +646,19 @@
             dma(()),
             dma(()),
             dma(()),
-            dma(()),
             dma((8,)),
             dma((8,)),
-            dma((4,)),
         ],
-        compiler_params=pltpu.CompilerParams(has_side_effects=True, collective_id=1),
+        compiler_params=pltpu.CompilerParams(
+            has_side_effects=True, collective_id=1, vmem_limit_bytes=24 << 20
+        ),
         name="cloud_step",
-    )(velocity, theta, vapour, radius_sq.T, multiplicity.T, counts, pairing, destination.T, *held)
+    )(*[
+        pltpu.with_memory_space_constraint(value, pltpu.HBM)
+        for value in (
+            velocity, theta, vapour, radius_sq.T, multiplicity.T, counts, pairing, destination.T, *held
+        )
+    ])
     return pl.pallas_call(
         final_kernel,
         out_shape=(
@@ -682,22 +667,20 @@
             shape(block, F32),
             shape((3, 32), F32),
         ),
-        in_specs=[ANY] * 6,
+        in_specs=[here] * 4,
         out_specs=(ANY,) * 4,
         scratch_shapes=[
-            vmem((5, DEV, 128), F32),
             vmem((3,) + block, F32),
-            vmem(block, F32),
-            vmem(block, F32),
-            vmem((8, 128), F32),
             vmem((3, 32), F32),
-            vmem((2, NZ, NZ), BF16),
             vmem((640, 128), F32),
-            dma((6,)),
-            dma((4,)),
+            dma((7,)),
         ],
+        compiler_params=pltpu.CompilerParams(vmem_limit_bytes=12 << 20),
         name="project",
-    )(modes, star, theta_new, vapour_new, moments, jnp.asarray(t["back"]))
+    )(
+        *[pltpu.with_memory_space_constraint(value, pltpu.VMEM) for value in (modes, advected, moments)],
+        jnp.asarray(t["back"]),
+    )
 
 
 def solution(mesh):

time: 35.4 us -> 34 us (0.960)
  Pallas kernels: 34.6 us -> 33.2 us
    pallas_call x1, Pallas kernels: 2.54 us -> 1.29 us  [shards(): pl.pallas_call(final_kernel, out_shape=(shape((3,) + block, F32), shape(b...]
where the time goes in v4:
time: 34 us; the launch traced here: 33.9 us
  Pallas kernels  33.2 us (98%)
  between operations  0.66 us (2%)
    pallas_call x1, Pallas kernels, shards(): pl.pallas_call(step_kernel, out_shape=(vmem((5, DEV, 128), F32), vmem((5,...  31.9 us
    pallas_call x1, Pallas kernels, shards(): pl.pallas_call(final_kernel, out_shape=(shape((3,) + block, F32), shape(b...  1.29 us

profile of v4, /device:TPU:1, one launch (start us, length us, event | category | flops | bytes accessed | tf_op | source)
XLA Modules:
  0.0 33.9 jit_solution(16644206199290973216)
XLA Ops:
  0.6 0.0 copy-start
  0.6 31.9 %cloud_step.1 = (f32[5,128,128]{2,1,0:T(8,128)S(1)}, f32[5,16,32,128]{3,2,1,0:T(8,128)S(1)}, f32[8,128]{1,0:T(8,128)S(1)}) custom-call(f32[3,16,32,128]{3,2,1,0:T(8,128)} %vel.1, f32[16,32,128]{2,1,0:T(8,128)} %theta.1, f32[16,32,128]{2,1,0:T(8,128)} %vapour.1, f32[32,64]{1,0:T(8,128)} %bitcast.3, f32[32,64]{1,0:T(8,128)} %bitcast.4, s32[32]{0:T(128)} %counts.1, ...), custom_call_target="tpu_custom_call" | custom-call | tf_op jit(solution)/shard_map/cloud_step/pallas_call | solution.py:606
  32.6 0.0 copy-done
  32.6 1.3 %project.1 = (f32[3,16,32,128]{3,2,1,0:T(8,128)}, f32[16,32,128]{2,1,0:T(8,128)}, f32[16,32,128]{2,1,0:T(8,128)}, f32[3,32]{1,0:T(4,128)}) custom-call(f32[5,128,128]{2,1,0:T(8,128)S(1)} %get-tuple-element.7.modes, f32[5,16,32,128]{3,2,1,0:T(8,128)S(1)} %get-tuple-element.8.ad, f32[8,128]{1,0:T(8,128)S(1)} %get-tuple-element.9.moments, ...), custom_call_target="tpu_custom_call" | custom-call | tf_op jit(solution)/shard_map/project/pallas_call | solution.py:662
Async XLA Ops:
  0.6 31.9 %copy-start = (bf16[2,128,128]{2,1,0:T(8,128)(2,1)S(1)}, bf16[2,128,128]{2,1,0:T(8,128)(2,1)}, u32[]{:S(2)}) copy-start(bf16[2,128,128]{2,1,0:T(8,128)(2,1)} %constant.26.clone.back) | copy-start | bytes 196612

commit v5 on v4

--- a/solution.py
+++ b/solution.py
@@ -100,15 +100,15 @@
         for j in range(32):
             box[column * 8 + j // 4, column * 32 + j] = 1.0
     return dict(
-        cosine=split_table(cosine),
-        first=split_table(np.stack(first)),
+        cosine=packed_left(cosine),
+        first=packed_left(np.stack(first)),
         ahead=split_table(ahead),
         behind=split_table(behind),
         last=split_table(np.stack(last)),
         turns=turns.astype(np.float32),
         wave_z=wave_z,
         box=box.astype(jnp.bfloat16),
-        back=split_table(back),
+        back=np.block([[*split_table(back)], [split_table(back)[0], np.zeros((NZ, NZ), jnp.bfloat16)]]),
     )
 
 
@@ -123,6 +123,26 @@
 
     (left_high, left_low), (right_high, right_low) = left, right
     return one(left_high, right_high) + (one(left_high, right_low) + one(left_low, right_high))
+
+
+def packed_left(table):
+    high, low = split_table(table)
+    return np.concatenate([high, low], axis=-1)
+
+
+def fold(wide):
+    return wide[:, :128] + wide[:, 128:]
+
+
+def packed_right(high, low):
+    zero = jnp.zeros_like(low)
+    return jnp.concatenate(
+        [jnp.concatenate([high, low], axis=1), jnp.concatenate([high, zero], axis=1)], axis=0
+    )
+
+
+def one_product(left, right, dims):
+    return lax.dot_general(left, right, (dims, ((), ())), preferred_element_type=F32)
 
 
 NN = ((1,), (0,))
@@ -339,7 +359,7 @@
             ad[f, x, 0:8, :] += c_south * yl[f, pl.ds(x, 1), :]
             ad[f, x, SY - 8 : SY, :] += c_north * yh[f, pl.ds(x, 1), :]
 
-    def block(c, carry):
+    def block(c):
         parts = []
         for i in range(4):
             x = c * 4 + i
@@ -349,14 +369,18 @@
             star_v = ad[1, x]
             star_u = ad[0, x]
             if i == 0:
-                last_u = jnp.where(c == 0, before_u[...], ad[0, jnp.maximum(x - 1, 0)])
+                last_u = before_u[...] if c == 0 else ad[0, x - 1]
             behind_v = jnp.where(row == 0, below_y[pl.ds(x, 1), :], pltpu.roll(star_v, 1, 0))
             below_w = jnp.where(lane == 0, 0.0, downward(star_w))
             parts.append((star_u - last_u) + (star_v - behind_v) + (star_w - below_w))
             last_u = star_u
         chunk = jnp.concatenate(parts, axis=0)
-        send1[c] = product((cosine[0], cosine[1]), halves(chunk), NT)
-        return carry
+        high, low = halves(chunk)
+        wide = jnp.concatenate(
+            [jnp.concatenate([high, high], axis=1), jnp.concatenate([low, jnp.zeros_like(low)], axis=1)],
+            axis=0,
+        )
+        send1[c] = fold(one_product(cosine[...], wide, NT))
 
     def scalars(c, carry):
         total = jnp.zeros((SY, NZ), F32)
@@ -368,7 +392,8 @@
         quad[c] = total
         return carry
 
-    lax.fori_loop(0, 4, block, 0)
+    for c in range(4):
+        block(c)
     pl.semaphore_wait(known.at[0], len(corners))
 
     def scatter(source, target_ref, send_sem, recv_sem):
@@ -460,7 +485,7 @@
     drained(send1, got1, r1_sem)
     z_re, z_im = [], []
     for c in range(4):
-        both = product((first[0, c], first[1, c]), halves(got1[c]), NN)
+        both = fold(one_product(first[c], packed_right(*halves(got1[c])), NN))
         z_re.append(both[:HALF])
         z_im.append(both[HALF:])
 
@@ -499,7 +524,9 @@
     edge = None
     for c in range(4):
         stacked = jnp.concatenate([v_re[c], v_im[c]], axis=0)
-        plane = product((last[0, c], last[1, c]), halves(stacked), NN)
+        high, low = halves(stacked)
+        wide = one_product(last[0, c], jnp.concatenate([high, low], axis=1), NN)
+        plane = fold(wide) + one_product(last[1, c], high, NN)
         send2[c] = plane
         if c == 0:
             next_x = pltpu.roll(plane, 120, 0)
@@ -571,7 +598,8 @@
     lane = lax.broadcasted_iota(jnp.int32, (SY, NZ), 1)
 
     def levels(c):
-        pressure[pl.ds(128 * c, 128), :] = product(halves(modes[c]), (back[0], back[1]), TN)
+        wide = one_product(jnp.concatenate(halves(modes[c]), axis=0), back[...], TN)
+        pressure[pl.ds(128 * c, 128), :] = fold(wide)
 
     levels(4)
     for c in (3, 2, 1, 0):

time: 34 us -> 33.1 us (0.974)
  Pallas kernels: 33.2 us -> 32.4 us
    pallas_call x1, Pallas kernels: 31.9 us -> 31.1 us  [shards(): pl.pallas_call(step_kernel, out_shape=(vmem((5, DEV, 128), F32), vmem((5,...]
where the time goes in v5:
time: 33.1 us; the launch traced here: 33 us
  Pallas kernels  32.4 us (98%)
  between operations  0.66 us (2%)
    pallas_call x1, Pallas kernels, shards(): pl.pallas_call(step_kernel, out_shape=(vmem((5, DEV, 128), F32), vmem((5,...  31.1 us
    pallas_call x1, Pallas kernels, shards(): pl.pallas_call(final_kernel, out_shape=(shape((3,) + block, F32), shape(b...  1.26 us

profile of v5, /device:TPU:1, one launch (start us, length us, event | category | flops | bytes accessed | tf_op | source)
XLA Modules:
  0.0 33.0 jit_solution(17985921869920895979)
XLA Ops:
  0.6 0.0 copy-start
  0.6 31.1 %cloud_step.1 = (f32[5,128,128]{2,1,0:T(8,128)S(1)}, f32[5,16,32,128]{3,2,1,0:T(8,128)S(1)}, f32[8,128]{1,0:T(8,128)S(1)}) custom-call(f32[3,16,32,128]{3,2,1,0:T(8,128)} %vel.1, f32[16,32,128]{2,1,0:T(8,128)} %theta.1, f32[16,32,128]{2,1,0:T(8,128)} %vapour.1, f32[32,64]{1,0:T(8,128)} %bitcast.3, f32[32,64]{1,0:T(8,128)} %bitcast.4, s32[32]{0:T(128)} %counts.1, ...), custom_call_target="tpu_custom_call" | custom-call | tf_op jit(solution)/shard_map/cloud_step/pallas_call | solution.py:634
  31.8 0.0 copy-done
  31.8 1.3 %project.1 = (f32[3,16,32,128]{3,2,1,0:T(8,128)}, f32[16,32,128]{2,1,0:T(8,128)}, f32[16,32,128]{2,1,0:T(8,128)}, f32[3,32]{1,0:T(4,128)}) custom-call(f32[5,128,128]{2,1,0:T(8,128)S(1)} %get-tuple-element.7.modes, f32[5,16,32,128]{3,2,1,0:T(8,128)S(1)} %get-tuple-element.8.ad, f32[8,128]{1,0:T(8,128)S(1)} %get-tuple-element.9.moments, ...), custom_call_target="tpu_custom_call" | custom-call | tf_op jit(solution)/shard_map/project/pallas_call | solution.py:690
Async XLA Ops:
  0.6 31.1 %copy-start = (bf16[256,256]{1,0:T(8,128)(2,1)S(1)}, bf16[256,256]{1,0:T(8,128)(2,1)}, u32[]{:S(2)}) copy-start(bf16[256,256]{1,0:T(8,128)(2,1)} %constant.26.clone.back) | copy-start | bytes 393220

commit v6 on v5

--- a/solution.py
+++ b/solution.py
@@ -30,17 +30,20 @@
 @functools.cache
 def send_order():
     hops = (0, 1, 2, 1)
-    peers = [(rx, ry) for rx in range(GX) for ry in range(GY) if rx or ry]
-    peers.sort(key=lambda p: -(hops[p[0] // 4] + hops[p[0] % 4] + hops[p[1] // 2]))
-    classes = {}
-    for p in peers:
-        classes.setdefault((p[0] // 4 > 2, p[0] % 4 > 2, p[1] // 2 > 2, p[1] % 2), []).append(p)
-    queues = list(classes.values())
-    order = []
-    while any(queues):
-        for queue in queues:
-            if queue:
-                order.append(queue.pop(0))
+    ways = ((0, 0), (1, 0), (1, 1), (0, 1))
+    left = [(k, i, j, n) for k in range(4) for i in range(4) for j in range(4) for n in range(2)][1:]
+    used, order = [0] * 6, []
+
+    def after(peer):
+        return [u + w for u, w in zip(used, sum((ways[step] for step in peer[:3]), ()))]
+
+    while left:
+        far = max(sum(hops[step] for step in peer[:3]) for peer in left)
+        ring = [peer for peer in left if sum(hops[step] for step in peer[:3]) == far]
+        best = min(ring, key=lambda peer: (max(after(peer)), sum(u * u for u in after(peer))))
+        used = after(best)
+        order.append(best)
+        left.remove(best)
     return tuple(order)
 
 
@@ -165,8 +168,6 @@
     me = gx * GY + gy
     east, west = lax.rem(gx + 1, GX), lax.rem(gx + GX - 1, GX)
     north, south = lax.rem(gy + 1, GY), lax.rem(gy + GY - 1, GY)
-    peers_x = [lax.rem(gx + r, GX) for r in range(GX)]
-    peers_y = [lax.rem(gy + r, GY) for r in range(GY)]
 
     loads = [
         pltpu.make_async_copy(vel, fp.at[pl.ds(0, 3), pl.ds(1, SX)], load_sem.at[0]),
@@ -194,12 +195,11 @@
 
     chip_z, chip_x, chip_y, core = gx // 4, lax.rem(gx, 4), gy // 2, lax.rem(gy, 2)
 
+    peers_x = [[lax.rem(chip_z + k, 4) * 4 + lax.rem(chip_x + i, 4) for i in range(4)] for k in range(4)]
+    peers_y = [[lax.rem(chip_y + j, 4) * 2 + lax.rem(core + n, 2) for n in range(2)] for j in range(4)]
+
     def away(step_z, step_x, step_y, step_core):
-        to_z, to_x, to_y = (
-            lax.rem(at + 4 + step, 4)
-            for at, step in ((chip_z, step_z), (chip_x, step_x), (chip_y, step_y))
-        )
-        return to_z * 4 + to_x, to_y * 2 + lax.rem(core + step_core, 2)
+        return peers_x[step_z % 4][step_x % 4], peers_y[step_y % 4][step_core]
 
     steps = [(k, i, j, n) for k in (0, 1, -1) for i in (1, -1, 0) for j in (1, -1, 0) for n in (0, 1)]
     around = [away(*step) for step in steps if any(step)]
@@ -214,29 +214,31 @@
             device_id=device, device_id_type=MESH,
         )
 
+    winds = fp.at[pl.ds(0, 3)]
     wind = [
-        remote(vel.at[:, SX - 1], fp.at[pl.ds(0, 3), 0], 0, (east, gy)),
-        remote(vel.at[:, 0], fp.at[pl.ds(0, 3), SX + 1], 1, (west, gy)),
-        remote(vel.at[0, SX - 2], xu2, 2, (east, gy)),
-        remote(vel.at[:, :, SY - 1], yl.at[pl.ds(0, 3)], 3, (gx, north)),
-        remote(vel.at[:, :, 0], yh.at[pl.ds(0, 3)], 4, (gx, south)),
-        remote(vel.at[1, :, SY - 2], yl.at[5], 5, (gx, north)),
-        remote(vel.at[0, SX - 1, pl.ds(SY - 1, 1)], corner.at[0, pl.ds(0, 1)], 6, (east, north)),
-        remote(vel.at[0, SX - 1, pl.ds(0, 1)], corner.at[1, pl.ds(0, 1)], 7, (east, south)),
-        remote(vel.at[1, SX - 1, pl.ds(SY - 1, 1)], corner.at[2, pl.ds(0, 1)], 8, (east, north)),
-        remote(vel.at[1, 0, pl.ds(SY - 1, 1)], corner.at[3, pl.ds(0, 1)], 9, (west, north)),
+        remote(winds.at[:, SX], fp.at[pl.ds(0, 3), 0], 0, (east, gy)),
+        remote(winds.at[:, 1], fp.at[pl.ds(0, 3), SX + 1], 1, (west, gy)),
+        remote(fp.at[0, SX - 1], xu2, 2, (east, gy)),
+        remote(winds.at[:, pl.ds(1, SX), SY - 1], yl.at[pl.ds(0, 3)], 3, (gx, north)),
+        remote(winds.at[:, pl.ds(1, SX), 0], yh.at[pl.ds(0, 3)], 4, (gx, south)),
+        remote(fp.at[1, pl.ds(1, SX), SY - 2], yl.at[5], 5, (gx, north)),
+        remote(fp.at[0, SX, pl.ds(SY - 1, 1)], corner.at[0, pl.ds(0, 1)], 6, (east, north)),
+        remote(fp.at[0, SX, pl.ds(0, 1)], corner.at[1, pl.ds(0, 1)], 7, (east, south)),
+        remote(fp.at[1, SX, pl.ds(SY - 1, 1)], corner.at[2, pl.ds(0, 1)], 8, (east, north)),
+        remote(fp.at[1, 1, pl.ds(SY - 1, 1)], corner.at[3, pl.ds(0, 1)], 9, (west, north)),
     ]
     air = [
-        remote(theta.at[SX - 1], fp.at[3, 0], 10, (east, gy)),
-        remote(vapour.at[SX - 1], fp.at[4, 0], 11, (east, gy)),
-        remote(theta.at[0], fp.at[3, SX + 1], 12, (west, gy)),
-        remote(vapour.at[0], fp.at[4, SX + 1], 13, (west, gy)),
-        remote(theta.at[:, SY - 1], yl.at[3], 14, (gx, north)),
-        remote(vapour.at[:, SY - 1], yl.at[4], 15, (gx, north)),
-        remote(theta.at[:, 0], yh.at[3], 16, (gx, south)),
-        remote(vapour.at[:, 0], yh.at[4], 17, (gx, south)),
+        remote(fp.at[3, SX], fp.at[3, 0], 10, (east, gy)),
+        remote(fp.at[4, SX], fp.at[4, 0], 11, (east, gy)),
+        remote(fp.at[3, 1], fp.at[3, SX + 1], 12, (west, gy)),
+        remote(fp.at[4, 1], fp.at[4, SX + 1], 13, (west, gy)),
+        remote(fp.at[3, pl.ds(1, SX), SY - 1], yl.at[3], 14, (gx, north)),
+        remote(fp.at[4, pl.ds(1, SX), SY - 1], yl.at[4], 15, (gx, north)),
+        remote(fp.at[3, pl.ds(1, SX), 0], yh.at[3], 16, (gx, south)),
+        remote(fp.at[4, pl.ds(1, SX), 0], yh.at[4], 17, (gx, south)),
     ]
     halo = wind + air
+    loads[0].wait()
     for copy in wind[6:] + wind[:6]:
         copy.start()
 
@@ -245,7 +247,7 @@
             pl.semaphore_signal(known.at[k], inc=1, device_id=device, device_id_type=MESH)
 
     pass_on(0, corners)
-    for copy in loads:
+    for copy in loads[1:]:
         copy.wait()
 
     row = lax.broadcasted_iota(jnp.int32, (SY, NZ), 0)
@@ -397,16 +399,13 @@
     pl.semaphore_wait(known.at[0], len(corners))
 
     def scatter(source, target_ref, send_sem, recv_sem):
-        def one(px, ry):
-            py = peers_y[ry]
+        for step_z, step_x, step_y, step_core in send_order():
+            px, py = peers_x[step_z][step_x], peers_y[step_y][step_core]
             pltpu.make_async_remote_copy(
                 src_ref=source.at[:, pl.ds(px * GY + py, 1), :],
                 dst_ref=target_ref.at[:, pl.ds(me, 1), :],
                 send_sem=send_sem, recv_sem=recv_sem, device_id=(px, py), device_id_type=MESH,
             ).start()
-
-        for rx, ry in send_order():
-            one(peers_x[rx], ry)
 
     def drained(source, target_ref, sem):
         count = pl.ds(0, DEV - 1)

time: 33.1 us -> 32.2 us (0.973)
  Pallas kernels: 32.4 us -> 31.4 us
    pallas_call x1, Pallas kernels: 31.1 us -> 30.1 us  [shards(): pl.pallas_call(step_kernel, out_shape=(vmem((5, DEV, 128), F32), vmem((5,...]
where the time goes in v6:
time: 32.2 us; the launch traced here: 32.1 us
  Pallas kernels  31.4 us (98%)
  between operations  0.66 us (2%)
    pallas_call x1, Pallas kernels, shards(): pl.pallas_call(step_kernel, out_shape=(vmem((5, DEV, 128), F32), vmem((5,...  30.1 us
    pallas_call x1, Pallas kernels, shards(): pl.pallas_call(final_kernel, out_shape=(shape((3,) + block, F32), shape(b...  1.26 us

profile of v6, /device:TPU:1, one launch (start us, length us, event | category | flops | bytes accessed | tf_op | source)
XLA Modules:
  0.0 32.1 jit_solution(7088622987670671563)
XLA Ops:
  0.6 0.0 copy-start
  0.6 30.1 %cloud_step.1 = (f32[5,128,128]{2,1,0:T(8,128)S(1)}, f32[5,16,32,128]{3,2,1,0:T(8,128)S(1)}, f32[8,128]{1,0:T(8,128)S(1)}) custom-call(f32[3,16,32,128]{3,2,1,0:T(8,128)} %vel.1, f32[16,32,128]{2,1,0:T(8,128)} %theta.1, f32[16,32,128]{2,1,0:T(8,128)} %vapour.1, f32[32,64]{1,0:T(8,128)} %bitcast.3, f32[32,64]{1,0:T(8,128)} %bitcast.4, s32[32]{0:T(128)} %counts.1, ...), custom_call_target="tpu_custom_call" | custom-call | tf_op jit(solution)/shard_map/cloud_step/pallas_call | solution.py:633
  30.8 0.0 copy-done
  30.8 1.3 %project.1 = (f32[3,16,32,128]{3,2,1,0:T(8,128)}, f32[16,32,128]{2,1,0:T(8,128)}, f32[16,32,128]{2,1,0:T(8,128)}, f32[3,32]{1,0:T(4,128)}) custom-call(f32[5,128,128]{2,1,0:T(8,128)S(1)} %get-tuple-element.7.modes, f32[5,16,32,128]{3,2,1,0:T(8,128)S(1)} %get-tuple-element.8.ad, f32[8,128]{1,0:T(8,128)S(1)} %get-tuple-element.9.moments, ...), custom_call_target="tpu_custom_call" | custom-call | tf_op jit(solution)/shard_map/project/pallas_call | solution.py:689
Async XLA Ops:
  0.6 30.2 %copy-start = (bf16[256,256]{1,0:T(8,128)(2,1)S(1)}, bf16[256,256]{1,0:T(8,128)(2,1)}, u32[]{:S(2)}) copy-start(bf16[256,256]{1,0:T(8,128)(2,1)} %constant.26.clone.back) | copy-start | bytes 393220

commit v7 on v6

--- a/solution.py
+++ b/solution.py
@@ -202,6 +202,7 @@
         return peers_x[step_z % 4][step_x % 4], peers_y[step_y % 4][step_core]
 
     steps = [(k, i, j, n) for k in (0, 1, -1) for i in (1, -1, 0) for j in (1, -1, 0) for n in (0, 1)]
+    steps.sort(key=lambda step: -sum(map(abs, step[:3])))
     around = [away(*step) for step in steps if any(step)]
     corners = [away(k, i, j, 0) for k in (1, -1) for i in (1, -1) for j in (1, -1)]
     for device in around:
@@ -290,6 +291,9 @@
         return carry
 
     lax.fori_loop(1, SX - 1, inner, 0)
+    for copy in air:
+        copy.start()
+
     for copy in drops:
         copy.wait()
     box_row = lax.broadcasted_iota(jnp.int32, (32, 32), 0)
@@ -321,8 +325,6 @@
         row_y0[pl.ds(x, 1), :] = fp[1, x + 1, 0:1, :]
     for copy in wind:
         copy.wait_recv()
-    for copy in air:
-        copy.start()
     advect_plane(0, (0, 1, 2))
     advect_plane(SX - 1, (0, 1, 2))
 

time: 32.2 us -> 31.8 us (0.988)
  Pallas kernels: 31.4 us -> 31 us
    pallas_call x1, Pallas kernels: 30.1 us -> 29.7 us  [shards(): pl.pallas_call(step_kernel, out_shape=(vmem((5, DEV, 128), F32), vmem((5,...]
where the time goes in v7:
time: 31.8 us; the launch traced here: 31.7 us
  Pallas kernels  31 us (97%)
  between operations  0.66 us (2%)
    pallas_call x1, Pallas kernels, shards(): pl.pallas_call(step_kernel, out_shape=(vmem((5, DEV, 128), F32), vmem((5,...  29.7 us
    pallas_call x1, Pallas kernels, shards(): pl.pallas_call(final_kernel, out_shape=(shape((3,) + block, F32), shape(b...  1.26 us

profile of v7, /device:TPU:1, one launch (start us, length us, event | category | flops | bytes accessed | tf_op | source)
XLA Modules:
  0.0 31.7 jit_solution(9610755288692194699)
XLA Ops:
  0.6 0.0 copy-start
  0.6 29.7 %cloud_step.1 = (f32[5,128,128]{2,1,0:T(8,128)S(1)}, f32[5,16,32,128]{3,2,1,0:T(8,128)S(1)}, f32[8,128]{1,0:T(8,128)S(1)}) custom-call(f32[3,16,32,128]{3,2,1,0:T(8,128)} %vel.1, f32[16,32,128]{2,1,0:T(8,128)} %theta.1, f32[16,32,128]{2,1,0:T(8,128)} %vapour.1, f32[32,64]{1,0:T(8,128)} %bitcast.3, f32[32,64]{1,0:T(8,128)} %bitcast.4, s32[32]{0:T(128)} %counts.1, ...), custom_call_target="tpu_custom_call" | custom-call | tf_op jit(solution)/shard_map/cloud_step/pallas_call | solution.py:635
  30.4 0.0 copy-done
  30.4 1.3 %project.1 = (f32[3,16,32,128]{3,2,1,0:T(8,128)}, f32[16,32,128]{2,1,0:T(8,128)}, f32[16,32,128]{2,1,0:T(8,128)}, f32[3,32]{1,0:T(4,128)}) custom-call(f32[5,128,128]{2,1,0:T(8,128)S(1)} %get-tuple-element.7.modes, f32[5,16,32,128]{3,2,1,0:T(8,128)S(1)} %get-tuple-element.8.ad, f32[8,128]{1,0:T(8,128)S(1)} %get-tuple-element.9.moments, ...), custom_call_target="tpu_custom_call" | custom-call | tf_op jit(solution)/shard_map/project/pallas_call | solution.py:691
Async XLA Ops:
  0.6 29.8 %copy-start = (bf16[256,256]{1,0:T(8,128)(2,1)S(1)}, bf16[256,256]{1,0:T(8,128)(2,1)}, u32[]{:S(2)}) copy-start(bf16[256,256]{1,0:T(8,128)(2,1)} %constant.26.clone.back) | copy-start | bytes 393220

commit v8 on v7

--- a/solution.py
+++ b/solution.py
@@ -107,7 +107,7 @@
         first=packed_left(np.stack(first)),
         ahead=split_table(ahead),
         behind=split_table(behind),
-        last=split_table(np.stack(last)),
+        last=np.concatenate(list(split_table(np.stack(last))), axis=1),
         turns=turns.astype(np.float32),
         wave_z=wave_z,
         box=box.astype(jnp.bfloat16),
@@ -323,34 +323,21 @@
 
     for x in (0, SX - 1):
         row_y0[pl.ds(x, 1), :] = fp[1, x + 1, 0:1, :]
-    for copy in wind:
+    for copy in wind[3:6]:
         copy.wait_recv()
-    advect_plane(0, (0, 1, 2))
-    advect_plane(SX - 1, (0, 1, 2))
-
-    speed = fp[0, 0]
-    c_east, c_west = coefficients(speed)
-    c_north, c_south = coefficients(fp[1, 0])
-    c_up, c_down, c_mid = vertical(fp[2, 0], lane)
-    above = jnp.where(row == SY - 1, corner[1, 0:1, :], pltpu.roll(speed, SY - 1, 0))
-    beneath = jnp.where(row == 0, corner[0, 0:1, :], pltpu.roll(speed, 1, 0))
-    before_u[...] = (
-        (c_mid * speed + c_east * fp[0, 1] + c_west * xu2[...])
-        + (c_north * above + c_south * beneath)
-        + (c_up * upward(speed) + c_down * downward(speed))
-    )
-    speed = yl[1]
+
+    speed_v = yl[1]
     row_x = lax.broadcasted_iota(jnp.int32, (SX, NZ), 0)
     lane_x = lax.broadcasted_iota(jnp.int32, (SX, NZ), 1)
     c_east, c_west = coefficients(yl[0])
-    c_north, c_south = coefficients(speed)
+    c_north, c_south = coefficients(speed_v)
     c_up, c_down, c_mid = vertical(yl[2], lane_x)
-    after = jnp.where(row_x == SX - 1, corner[3, 0:1, :], pltpu.roll(speed, SX - 1, 0))
-    before = jnp.where(row_x == 0, corner[2, 0:1, :], pltpu.roll(speed, 1, 0))
+    after = jnp.where(row_x == SX - 1, 0.0, pltpu.roll(speed_v, SX - 1, 0))
+    before = jnp.where(row_x == 0, 0.0, pltpu.roll(speed_v, 1, 0))
     below_y[...] = (
-        (c_mid * speed + c_east * after + c_west * before)
+        (c_mid * speed_v + c_east * after + c_west * before)
         + (c_north * row_y0[...] + c_south * yl[5])
-        + (c_up * upward(speed) + c_down * downward(speed))
+        + (c_up * upward(speed_v) + c_down * downward(speed_v))
     )
     fetches[0].wait()
 
@@ -367,7 +354,8 @@
         parts = []
         for i in range(4):
             x = c * 4 + i
-            border(x, (0, 1, 2))
+            if x != 3:
+                border(x, (0, 1, 2))
             star_w = ad[2, x] + 0.1 * fp[3, x + 1]
             ad[2, x] = star_w
             star_v = ad[1, x]
@@ -396,8 +384,34 @@
         quad[c] = total
         return carry
 
-    for c in range(4):
-        block(c)
+    border(3, (0, 1, 2))
+    block(1)
+    block(2)
+    for copy in wind[:3]:
+        copy.wait_recv()
+    advect_plane(0, (0, 1, 2))
+    advect_plane(SX - 1, (0, 1, 2))
+
+    for copy in wind[6:]:
+        copy.wait_recv()
+    _, end_west = coefficients(yl[0, 0:1, :])
+    end_east, _ = coefficients(yl[0, SX - 1 : SX, :])
+    below_y[0:1, :] += end_west * corner[2, 0:1, :]
+    below_y[SX - 1 : SX, :] += end_east * corner[3, 0:1, :]
+
+    speed = fp[0, 0]
+    c_east, c_west = coefficients(speed)
+    c_north, c_south = coefficients(fp[1, 0])
+    c_up, c_down, c_mid = vertical(fp[2, 0], lane)
+    above = jnp.where(row == SY - 1, corner[1, 0:1, :], pltpu.roll(speed, SY - 1, 0))
+    beneath = jnp.where(row == 0, corner[0, 0:1, :], pltpu.roll(speed, 1, 0))
+    before_u[...] = (
+        (c_mid * speed + c_east * fp[0, 1] + c_west * xu2[...])
+        + (c_north * above + c_south * beneath)
+        + (c_up * upward(speed) + c_down * downward(speed))
+    )
+    block(0)
+    block(3)
     pl.semaphore_wait(known.at[0], len(corners))
 
     def scatter(source, target_ref, send_sem, recv_sem):
@@ -505,29 +519,36 @@
             [s02i + s13i, d02i + d13r, s02i - s13i, d02i - d13r],
         )
 
+    def stacked_product(values, table):
+        high, low = halves(values)
+        both = one_product(jnp.concatenate([high, low], axis=0), table[0], NN)
+        rows = values.shape[0]
+        return both[:rows] + (both[rows:] + one_product(high, table[1], NN))
+
     q_re, q_im = butterfly(z_re, z_im, -1)
-    re, im = jnp.concatenate(q_re, axis=0), jnp.concatenate(q_im, axis=0)
-    turn_cos, turn_sin = turns[0], turns[1]
-    joined = jnp.concatenate([re * turn_cos + im * turn_sin, im * turn_cos - re * turn_sin], axis=1)
-    spectrum = product(halves(joined), (ahead[0], ahead[1]), NN)
-    eigen = turns[2] + wave[pl.ds(me, 1), :]
-    inverse = jnp.where(eigen == 0.0, 0.0, 1.0 / jnp.where(eigen == 0.0, 1.0, eigen))
-    solved = spectrum * jnp.concatenate([inverse, inverse], axis=1)
-    turned = product(halves(solved), (behind[0], behind[1]), NN)
-    re, im = turned[:, :128], turned[:, 128:]
-    back_re, back_im = re * turn_cos - im * turn_sin, im * turn_cos + re * turn_sin
-    v_re, v_im = butterfly(
-        [back_re[HALF * q : HALF * (q + 1)] for q in range(4)],
-        [back_im[HALF * q : HALF * (q + 1)] for q in range(4)],
-        1,
-    )
+    back_re, back_im = [], []
+    for q in range(0, 4, 2):
+        part = pl.ds(HALF * q, HALF * 2)
+        re, im = (jnp.concatenate(side[q : q + 2], axis=0) for side in (q_re, q_im))
+        turn_cos, turn_sin = turns[0, part, :], turns[1, part, :]
+        joined = jnp.concatenate([re * turn_cos + im * turn_sin, im * turn_cos - re * turn_sin], axis=1)
+        spectrum = stacked_product(joined, ahead)
+        eigen = turns[2, part, :] + wave[pl.ds(me, 1), :]
+        inverse = jnp.where(eigen == 0.0, 0.0, 1.0 / jnp.where(eigen == 0.0, 1.0, eigen))
+        turned = stacked_product(spectrum * jnp.concatenate([inverse, inverse], axis=1), behind)
+        re, im = turned[:, :128], turned[:, 128:]
+        turned_re, turned_im = re * turn_cos - im * turn_sin, im * turn_cos + re * turn_sin
+        for k in range(2):
+            back_re.append(turned_re[HALF * k : HALF * (k + 1)])
+            back_im.append(turned_im[HALF * k : HALF * (k + 1)])
+    v_re, v_im = butterfly(back_re, back_im, 1)
     wide_lane = lax.broadcasted_iota(jnp.int32, (128, 128), 1)
     edge = None
     for c in range(4):
         stacked = jnp.concatenate([v_re[c], v_im[c]], axis=0)
         high, low = halves(stacked)
-        wide = one_product(last[0, c], jnp.concatenate([high, low], axis=1), NN)
-        plane = fold(wide) + one_product(last[1, c], high, NN)
+        wide = one_product(last[c], jnp.concatenate([high, low], axis=1), NN)
+        plane = wide[:128, :128] + (wide[:128, 128:] + wide[128:, :128])
         send2[c] = plane
         if c == 0:
             next_x = pltpu.roll(plane, 120, 0)

time: 31.8 us -> 31.6 us (level)
  no operation moved by 1% of the time
where the time goes in v8:
time: 31.6 us; the launch traced here: 31.5 us
  Pallas kernels  30.8 us (97%)
  between operations  0.66 us (2%)
    pallas_call x1, Pallas kernels, shards(): pl.pallas_call(step_kernel, out_shape=(vmem((5, DEV, 128), F32), vmem((5,...  29.6 us
    pallas_call x1, Pallas kernels, shards(): pl.pallas_call(final_kernel, out_shape=(shape((3,) + block, F32), shape(b...  1.26 us

profile of v8, /device:TPU:1, one launch (start us, length us, event | category | flops | bytes accessed | tf_op | source)
XLA Modules:
  0.0 31.5 jit_solution(9435386575755819141)
XLA Ops:
  0.6 0.0 copy-start
  0.6 29.6 %cloud_step.1 = (f32[5,128,128]{2,1,0:T(8,128)S(1)}, f32[5,16,32,128]{3,2,1,0:T(8,128)S(1)}, f32[8,128]{1,0:T(8,128)S(1)}) custom-call(f32[3,16,32,128]{3,2,1,0:T(8,128)} %vel.1, f32[16,32,128]{2,1,0:T(8,128)} %theta.1, f32[16,32,128]{2,1,0:T(8,128)} %vapour.1, f32[32,64]{1,0:T(8,128)} %bitcast.3, f32[32,64]{1,0:T(8,128)} %bitcast.4, s32[32]{0:T(128)} %counts.1, ...), custom_call_target="tpu_custom_call" | custom-call | tf_op jit(solution)/shard_map/cloud_step/pallas_call | solution.py:656
  30.2 0.0 copy-done
  30.2 1.3 %project.1 = (f32[3,16,32,128]{3,2,1,0:T(8,128)}, f32[16,32,128]{2,1,0:T(8,128)}, f32[16,32,128]{2,1,0:T(8,128)}, f32[3,32]{1,0:T(4,128)}) custom-call(f32[5,128,128]{2,1,0:T(8,128)S(1)} %get-tuple-element.7.modes, f32[5,16,32,128]{3,2,1,0:T(8,128)S(1)} %get-tuple-element.8.ad, f32[8,128]{1,0:T(8,128)S(1)} %get-tuple-element.9.moments, ...), custom_call_target="tpu_custom_call" | custom-call | tf_op jit(solution)/shard_map/project/pallas_call | solution.py:712
Async XLA Ops:
  0.6 29.6 %copy-start = (bf16[256,256]{1,0:T(8,128)(2,1)S(1)}, bf16[256,256]{1,0:T(8,128)(2,1)}, u32[]{:S(2)}) copy-start(bf16[256,256]{1,0:T(8,128)(2,1)} %constant.26.clone.back) | copy-start | bytes 393220

commit v9 on v8

--- a/solution.py
+++ b/solution.py
@@ -201,7 +201,9 @@
     def away(step_z, step_x, step_y, step_core):
         return peers_x[step_z % 4][step_x % 4], peers_y[step_y % 4][step_core]
 
-    steps = [(k, i, j, n) for k in (0, 1, -1) for i in (1, -1, 0) for j in (1, -1, 0) for n in (0, 1)]
+    cube = [(k, i, j) for k in (0, 1, -1) for i in (1, -1, 0) for j in (1, -1, 0)]
+    spare = [(k, 0, -k) for k in (1, -1)] + [(k, -k, j) for k in (1, -1) for j in (1, -1, 0)]
+    steps = [(*step, n) for step in cube for n in (0, 1) if n == 0 or step not in spare]
     steps.sort(key=lambda step: -sum(map(abs, step[:3])))
     around = [away(*step) for step in steps if any(step)]
     corners = [away(k, i, j, 0) for k in (1, -1) for i in (1, -1) for j in (1, -1)]

time: 31.6 us -> 31.6 us (level)
  no operation moved by 1% of the time
where the time goes in v9:
time: 31.6 us; the launch traced here: 31.5 us
  Pallas kernels  30.8 us (97%)
  between operations  0.66 us (2%)
    pallas_call x1, Pallas kernels, shards(): pl.pallas_call(step_kernel, out_shape=(vmem((5, DEV, 128), F32), vmem((5,...  29.6 us
    pallas_call x1, Pallas kernels, shards(): pl.pallas_call(final_kernel, out_shape=(shape((3,) + block, F32), shape(b...  1.26 us

profile of v9, /device:TPU:1, one launch (start us, length us, event | category | flops | bytes accessed | tf_op | source)
XLA Modules:
  0.0 31.5 jit_solution(14608310547822393443)
XLA Ops:
  0.6 0.0 copy-start
  0.6 29.6 %cloud_step.1 = (f32[5,128,128]{2,1,0:T(8,128)S(1)}, f32[5,16,32,128]{3,2,1,0:T(8,128)S(1)}, f32[8,128]{1,0:T(8,128)S(1)}) custom-call(f32[3,16,32,128]{3,2,1,0:T(8,128)} %vel.1, f32[16,32,128]{2,1,0:T(8,128)} %theta.1, f32[16,32,128]{2,1,0:T(8,128)} %vapour.1, f32[32,64]{1,0:T(8,128)} %bitcast.3, f32[32,64]{1,0:T(8,128)} %bitcast.4, s32[32]{0:T(128)} %counts.1, ...), custom_call_target="tpu_custom_call" | custom-call | tf_op jit(solution)/shard_map/cloud_step/pallas_call | solution.py:658
  30.2 0.0 copy-done
  30.2 1.3 %project.1 = (f32[3,16,32,128]{3,2,1,0:T(8,128)}, f32[16,32,128]{2,1,0:T(8,128)}, f32[16,32,128]{2,1,0:T(8,128)}, f32[3,32]{1,0:T(4,128)}) custom-call(f32[5,128,128]{2,1,0:T(8,128)S(1)} %get-tuple-element.7.modes, f32[5,16,32,128]{3,2,1,0:T(8,128)S(1)} %get-tuple-element.8.ad, f32[8,128]{1,0:T(8,128)S(1)} %get-tuple-element.9.moments, ...), custom_call_target="tpu_custom_call" | custom-call | tf_op jit(solution)/shard_map/project/pallas_call | solution.py:714
Async XLA Ops:
  0.6 29.6 %copy-start = (bf16[256,256]{1,0:T(8,128)(2,1)S(1)}, bf16[256,256]{1,0:T(8,128)(2,1)}, u32[]{:S(2)}) copy-start(bf16[256,256]{1,0:T(8,128)(2,1)} %constant.26.clone.back) | copy-start | bytes 393220

commit v10 on v7

--- a/solution.py
+++ b/solution.py
@@ -107,7 +107,7 @@
         first=packed_left(np.stack(first)),
         ahead=split_table(ahead),
         behind=split_table(behind),
-        last=split_table(np.stack(last)),
+        last=np.concatenate(list(split_table(np.stack(last))), axis=1),
         turns=turns.astype(np.float32),
         wave_z=wave_z,
         box=box.astype(jnp.bfloat16),
@@ -505,29 +505,36 @@
             [s02i + s13i, d02i + d13r, s02i - s13i, d02i - d13r],
         )
 
+    def stacked_product(values, table):
+        high, low = halves(values)
+        both = one_product(jnp.concatenate([high, low], axis=0), table[0], NN)
+        rows = values.shape[0]
+        return both[:rows] + (both[rows:] + one_product(high, table[1], NN))
+
     q_re, q_im = butterfly(z_re, z_im, -1)
-    re, im = jnp.concatenate(q_re, axis=0), jnp.concatenate(q_im, axis=0)
-    turn_cos, turn_sin = turns[0], turns[1]
-    joined = jnp.concatenate([re * turn_cos + im * turn_sin, im * turn_cos - re * turn_sin], axis=1)
-    spectrum = product(halves(joined), (ahead[0], ahead[1]), NN)
-    eigen = turns[2] + wave[pl.ds(me, 1), :]
-    inverse = jnp.where(eigen == 0.0, 0.0, 1.0 / jnp.where(eigen == 0.0, 1.0, eigen))
-    solved = spectrum * jnp.concatenate([inverse, inverse], axis=1)
-    turned = product(halves(solved), (behind[0], behind[1]), NN)
-    re, im = turned[:, :128], turned[:, 128:]
-    back_re, back_im = re * turn_cos - im * turn_sin, im * turn_cos + re * turn_sin
-    v_re, v_im = butterfly(
-        [back_re[HALF * q : HALF * (q + 1)] for q in range(4)],
-        [back_im[HALF * q : HALF * (q + 1)] for q in range(4)],
-        1,
-    )
+    back_re, back_im = [], []
+    for q in range(0, 4, 2):
+        part = pl.ds(HALF * q, HALF * 2)
+        re, im = (jnp.concatenate(side[q : q + 2], axis=0) for side in (q_re, q_im))
+        turn_cos, turn_sin = turns[0, part, :], turns[1, part, :]
+        joined = jnp.concatenate([re * turn_cos + im * turn_sin, im * turn_cos - re * turn_sin], axis=1)
+        spectrum = stacked_product(joined, ahead)
+        eigen = turns[2, part, :] + wave[pl.ds(me, 1), :]
+        inverse = jnp.where(eigen == 0.0, 0.0, 1.0 / jnp.where(eigen == 0.0, 1.0, eigen))
+        turned = stacked_product(spectrum * jnp.concatenate([inverse, inverse], axis=1), behind)
+        re, im = turned[:, :128], turned[:, 128:]
+        turned_re, turned_im = re * turn_cos - im * turn_sin, im * turn_cos + re * turn_sin
+        for k in range(2):
+            back_re.append(turned_re[HALF * k : HALF * (k + 1)])
+            back_im.append(turned_im[HALF * k : HALF * (k + 1)])
+    v_re, v_im = butterfly(back_re, back_im, 1)
     wide_lane = lax.broadcasted_iota(jnp.int32, (128, 128), 1)
     edge = None
     for c in range(4):
         stacked = jnp.concatenate([v_re[c], v_im[c]], axis=0)
         high, low = halves(stacked)
-        wide = one_product(last[0, c], jnp.concatenate([high, low], axis=1), NN)
-        plane = fold(wide) + one_product(last[1, c], high, NN)
+        wide = one_product(last[c], jnp.concatenate([high, low], axis=1), NN)
+        plane = wide[:128, :128] + (wide[:128, 128:] + wide[128:, :128])
         send2[c] = plane
         if c == 0:
             next_x = pltpu.roll(plane, 120, 0)

time: 31.8 us -> 31.7 us (level)
  no operation moved by 1% of the time
where the time goes in v10:
time: 31.7 us; the launch traced here: 31.6 us
  Pallas kernels  30.9 us (97%)
  between operations  0.66 us (2%)
    pallas_call x1, Pallas kernels, shards(): pl.pallas_call(step_kernel, out_shape=(vmem((5, DEV, 128), F32), vmem((5,...  29.7 us
    pallas_call x1, Pallas kernels, shards(): pl.pallas_call(final_kernel, out_shape=(shape((3,) + block, F32), shape(b...  1.26 us

profile of v10, /device:TPU:1, one launch (start us, length us, event | category | flops | bytes accessed | tf_op | source)
XLA Modules:
  0.0 31.6 jit_solution(11957760260388296024)
XLA Ops:
  0.6 0.0 copy-start
  0.6 29.7 %cloud_step.1 = (f32[5,128,128]{2,1,0:T(8,128)S(1)}, f32[5,16,32,128]{3,2,1,0:T(8,128)S(1)}, f32[8,128]{1,0:T(8,128)S(1)}) custom-call(f32[3,16,32,128]{3,2,1,0:T(8,128)} %vel.1, f32[16,32,128]{2,1,0:T(8,128)} %theta.1, f32[16,32,128]{2,1,0:T(8,128)} %vapour.1, f32[32,64]{1,0:T(8,128)} %bitcast.3, f32[32,64]{1,0:T(8,128)} %bitcast.4, s32[32]{0:T(128)} %counts.1, ...), custom_call_target="tpu_custom_call" | custom-call | tf_op jit(solution)/shard_map/cloud_step/pallas_call | solution.py:642
  30.3 0.0 copy-done
  30.3 1.3 %project.1 = (f32[3,16,32,128]{3,2,1,0:T(8,128)}, f32[16,32,128]{2,1,0:T(8,128)}, f32[16,32,128]{2,1,0:T(8,128)}, f32[3,32]{1,0:T(4,128)}) custom-call(f32[5,128,128]{2,1,0:T(8,128)S(1)} %get-tuple-element.7.modes, f32[5,16,32,128]{3,2,1,0:T(8,128)S(1)} %get-tuple-element.8.ad, f32[8,128]{1,0:T(8,128)S(1)} %get-tuple-element.9.moments, ...), custom_call_target="tpu_custom_call" | custom-call | tf_op jit(solution)/shard_map/project/pallas_call | solution.py:698
Async XLA Ops:
  0.6 29.7 %copy-start = (bf16[256,256]{1,0:T(8,128)(2,1)S(1)}, bf16[256,256]{1,0:T(8,128)(2,1)}, u32[]{:S(2)}) copy-start(bf16[256,256]{1,0:T(8,128)(2,1)} %constant.26.clone.back) | copy-start | bytes 393220
